TPU v7x, 32 devices: a whole 2x2x4 slice. The times are simulated.
32 devices in a mesh: dp: 8 (over y, x, core), mem: 4 (over z).
Axes of the slice: x: 2, y: 2, z: 4, core: 2. Of those that a mesh axis runs over, the one named last changes fastest.
Arguments:
- target_in: bfloat16 [2, 32, 256, 1024], P(None, ('dp', 'mem')), may hold values from -45 to 45
- memory: bfloat16 [2, 32, 1024, 1024], P(None, 'dp', 'mem'), may hold values from -6 to 6
- target_len: int32 [2, 32], P(None, ('dp', 'mem')), may hold values from 64 to 256, as said below
- mem_len: int32 [2, 32], P(None, ('dp', 'mem')), may hold values from 512 to 1024, as said below
- cotangent: bfloat16 [2, 32, 256, 1024], P(None, ('dp', 'mem')), may hold values from -6 to 6
- gain_self: float32 [1024], replicated, may hold values from 0.5 to 1.5
- gain_cross: float32 [1024], replicated, may hold values from 0.5 to 1.5
- gain_ffn: float32 [1024], replicated, may hold values from 0.5 to 1.5
- rel_table: float32 [32, 16], replicated, may hold values from -4 to 4
- w_query: bfloat16 [1024, 1024], replicated, may hold values from -0.0234375 to 0.0234375
- w_key: bfloat16 [1024, 512], replicated, may hold values from -0.1875 to 0.1875
- w_value: bfloat16 [1024, 512], replicated, may hold values from -0.1875 to 0.1875
- w_out: bfloat16 [1024, 1024], replicated, may hold values from -1.5 to 1.5
- c_query: bfloat16 [1024, 1024], replicated, may hold values from -0.0234375 to 0.0234375
- c_key: bfloat16 [1024, 512], replicated, may hold values from -0.1875 to 0.1875
- c_value: bfloat16 [1024, 512], replicated, may hold values from -0.1875 to 0.1875
- c_out: bfloat16 [1024, 1024], replicated, may hold values from -3 to 3
- w_gate: bfloat16 [1024, 2816], replicated, may hold values from -0.1875 to 0.1875
- w_up: bfloat16 [1024, 2816], replicated, may hold values from -0.1875 to 0.1875
- w_down: bfloat16 [2816, 1024], replicated, may hold values from -0.109375 to 0.109375
Outputs:
- out: bfloat16 [2, 32, 256, 1024], P(None, ('dp', 'mem'))
- target_grad: bfloat16 [2, 32, 256, 1024], P(None, ('dp', 'mem'))
- memory_grad: bfloat16 [2, 32, 1024, 1024], P(None, 'dp', 'mem')
- grad_gain_self: float32 [1024], replicated
- grad_gain_cross: float32 [1024], replicated
- grad_gain_ffn: float32 [1024], replicated
- grad_rel_table: float32 [32, 16], replicated
- grad_w_query: float32 [1024, 1024], P(('dp', 'mem'))
- grad_w_key: float32 [1024, 512], P(('dp', 'mem'))
- grad_w_value: float32 [1024, 512], P(('dp', 'mem'))
- grad_w_out: float32 [1024, 1024], P(('dp', 'mem'))
- grad_c_query: float32 [1024, 1024], P(('dp', 'mem'))
- grad_c_key: float32 [1024, 512], P(('dp', 'mem'))
- grad_c_value: float32 [1024, 512], P(('dp', 'mem'))
- grad_c_out: float32 [1024, 1024], P(('dp', 'mem'))
- grad_w_gate: float32 [1024, 2816], P(('dp', 'mem'))
- grad_w_up: float32 [1024, 2816], P(('dp', 'mem'))
- grad_w_down: float32 [2816, 1024], P(('dp', 'mem'))
Inputs may be any that keep to these rules, and one draw needn't show every extreme that they name: `target_len`: in every micro-batch one sequence has exactly 256 live target positions and another exactly a quarter of 256. `mem_len`: in every micro-batch one sequence has exactly 1024 live memory positions and another exactly half of 1024.
All inputs are finite; a program needn't handle non-finite values.
Results may differ from a plain program's by a relative error of at most 0.019.
Values may be sent and summed in bfloat16 or wider, within the bound.
No kernel may reach another device: no remote copies, remote signals or barrier semaphores. Data moves between devices by JAX's collectives and lax.ppermute only.
A program may use at most 384 MiB of HBM per device.

v0:
```python
import functools

import jax
import jax.numpy as jnp
import numpy as np
from jax import lax
from jax.experimental import pallas as pl
from jax.experimental.pallas import tpu as pltpu
from jax.sharding import PartitionSpec as P


QUERY_HEADS = 16
HEAD_SIZE = 64
KEY_VALUE_HEADS = 8
NB = 32
MAXD = 128
SHARED = QUERY_HEADS // KEY_VALUE_HEADS
PAIR = 2
PAIRS = KEY_VALUE_HEADS // PAIR
STEP_HEADS = PAIR * SHARED

EPSILON = 1e-06
MASKED = -1e30
EXACT_PRECISION = lax.Precision.HIGHEST


def bucket_index(length):
    half = NB // 2
    distance = np.arange(length)
    spread = np.floor(np.log(np.maximum(distance, half) / half) / np.log(MAXD / half) * half)
    return np.where(distance < half, distance, np.minimum(spread + half, NB - 1)).astype(np.int64)


def bucket_onehot(length):
    chosen = bucket_index(length)
    return np.where(chosen[None, :] == np.arange(NB)[:, None], 1.0, 0.0).astype(np.float32)


def inverse_rms(rows):
    return lax.rsqrt(jnp.mean(rows * rows, axis=-1, keepdims=True) + EPSILON)


def normed(rows, gain):
    return (rows * inverse_rms(rows) * gain).astype(jnp.bfloat16)


def norm_back(rows, gain, gradient):
    scale = inverse_rms(rows)
    scaled = gradient * gain
    shared = jnp.mean(scaled * rows, axis=-1, keepdims=True)
    part_rows = scale * scaled - rows * (scale * scale * scale * shared)
    return part_rows, jnp.sum(gradient * rows * scale, axis=0)


def dot32(left, right, dims):
    return lax.dot_general(left, right, (dims, ((), ())), preferred_element_type=jnp.float32)


def multiply(left, right):
    return dot32(left, right, ((1,), (0,)))


def outer_sum(left, right):
    return dot32(left, right, ((0,), (0,)))


def times_transposed(left, right):
    return dot32(left, right, ((1,), (1,)))


def head_rows(ref_rows, key_head):
    first = key_head * SHARED * HEAD_SIZE
    return jnp.concatenate(
        [ref_rows[:, first + i * HEAD_SIZE : first + (i + 1) * HEAD_SIZE] for i in range(SHARED)],
        axis=0,
    )


def head_columns(rows, length):
    return [rows[i * length : (i + 1) * length] for i in range(SHARED)]


def store_log_totals(lse_ref, columns):
    length = columns[0].shape[0]
    lane = lax.broadcasted_iota(jnp.int32, (length, 128), 1)
    packed = jnp.zeros((length, 128), jnp.float32)
    for index, column in enumerate(columns):
        packed = jnp.where(lane == index, column, packed)
    lse_ref[0, 0] = jnp.transpose(packed)[:8]


def self_forward_kernel(count_ref, q_ref, k_ref, v_ref, base_ref, out_ref, lse_ref):
    length = q_ref.shape[0]
    count = count_ref[pl.program_id(0)]
    row = lax.broadcasted_iota(jnp.int32, (length, length), 0)
    column = lax.broadcasted_iota(jnp.int32, (length, length), 1)
    keep = (column <= row) & (column < count)
    keep = jnp.concatenate([keep.astype(jnp.float32)] * SHARED, axis=0) > 0.5
    outs, totals = [], []
    for j in range(PAIR):
        queries = head_rows(q_ref, j)
        keys = k_ref[:, j * HEAD_SIZE : (j + 1) * HEAD_SIZE]
        values = v_ref[:, j * HEAD_SIZE : (j + 1) * HEAD_SIZE]
        bias = jnp.concatenate(
            [
                pltpu.roll(
                    jnp.broadcast_to(base_ref[0, j * SHARED + i : j * SHARED + i + 1, :], (length, length)),
                    0,
                    1,
                    stride=1,
                    stride_axis=0,
                )
                for i in range(SHARED)
            ],
            axis=0,
        )
        scores = jnp.where(keep, times_transposed(queries, keys) + bias, MASKED)
        highest = jnp.max(scores, axis=-1, keepdims=True)
        terms = jnp.exp(scores - highest)
        total = jnp.sum(terms, axis=-1, keepdims=True)
        mixed = multiply(terms.astype(jnp.bfloat16), values) / total
        outs += head_columns(mixed, length)
        totals += head_columns(highest + jnp.log(total), length)
    out_ref[...] = jnp.concatenate(outs, axis=1).astype(jnp.bfloat16)
    store_log_totals(lse_ref, totals)


def diagonal_sums(square):
    length = square.shape[0]
    group = 8
    total = square[:group]
    for first in range(group, length, group):
        total = total + pltpu.roll(square[first : first + group], length - first, 1)
    row = lax.broadcasted_iota(jnp.int32, (group, length), 0)
    sums = jnp.where(row == 0, total, 0.0)
    for r in range(1, group):
        sums = sums + jnp.where(row == r, pltpu.roll(total, length - r, 1), 0.0)
    return jnp.sum(sums, axis=0, keepdims=True)


def self_backward_kernel(
    count_ref, q_ref, k_ref, v_ref, g_ref, lse_ref, base_ref, dq_ref, dk_ref, dv_ref, diag_ref
):
    length = q_ref.shape[0]
    count = count_ref[pl.program_id(0)]
    row = lax.broadcasted_iota(jnp.int32, (length, length), 0)
    column = lax.broadcasted_iota(jnp.int32, (length, length), 1)
    keep = (row <= column) & (row < count)
    dqs, dks, dvs, diagonals = [], [], [], []
    for j in range(PAIR):
        queries = head_rows(q_ref, j)
        gradient = head_rows(g_ref, j)
        keys = k_ref[:, j * HEAD_SIZE : (j + 1) * HEAD_SIZE]
        values = v_ref[:, j * HEAD_SIZE : (j + 1) * HEAD_SIZE]
        scores_all = times_transposed(keys, queries)
        grad_all = times_transposed(values, gradient)
        weights, score_grads = [], []
        for i in range(SHARED):
            h = j * SHARED + i
            bias = pltpu.roll(
                jnp.broadcast_to(base_ref[0, h : h + 1, :], (length, length)),
                0,
                1,
                stride=1,
                stride_axis=0,
            )
            scores = scores_all[:, i * length : (i + 1) * length] + bias
            scores = jnp.where(keep, scores, MASKED)
            probs = jnp.exp(scores - lse_ref[0, 0, h : h + 1, :])
            weights.append(probs.astype(jnp.bfloat16))
            product = probs * grad_all[:, i * length : (i + 1) * length]
            centre = jnp.sum(product, axis=0, keepdims=True)
            score_grad = (product - probs * centre).astype(jnp.bfloat16)
            score_grads.append(score_grad)
            diagonals.append(diagonal_sums(score_grad.astype(jnp.float32)))
        weights = jnp.concatenate(weights, axis=1)
        score_grads = jnp.concatenate(score_grads, axis=1)
        dvs.append(multiply(weights, gradient))
        dks.append(multiply(score_grads, queries))
        dq = jnp.transpose(outer_sum(keys, score_grads))
        dqs += head_columns(dq, length)
    dq_ref[...] = jnp.concatenate(dqs, axis=1).astype(jnp.bfloat16)
    dk_ref[...] = jnp.concatenate(dks, axis=1).astype(jnp.bfloat16)
    dv_ref[...] = jnp.concatenate(dvs, axis=1).astype(jnp.bfloat16)
    diag_ref[0, 0] = jnp.concatenate(diagonals, axis=0)


def cross_forward_kernel(chunks, count_ref, base_ref, q_ref, *refs):
    k_refs, v_refs = refs[:chunks], refs[chunks : 2 * chunks]
    out_ref, lse_ref, score_ref = refs[2 * chunks :]
    length, rows = q_ref.shape[0], k_refs[0].shape[1]
    count = count_ref[pl.program_id(0)]
    column = lax.broadcasted_iota(jnp.int32, (1, rows), 1)
    outs, totals = [], []
    for j in range(PAIR):
        queries = head_rows(q_ref, j)
        highest = None
        for c in range(chunks):
            keys = k_refs[c][0, :, j * HEAD_SIZE : (j + 1) * HEAD_SIZE]
            scores = jnp.where(
                column + base_ref[c] < count, times_transposed(queries, keys), MASKED
            )
            score_ref[c] = scores
            top = jnp.max(scores, axis=-1, keepdims=True)
            highest = top if highest is None else jnp.maximum(highest, top)
        total, mixed = 0.0, 0.0
        for c in range(chunks):
            values = v_refs[c][0, :, j * HEAD_SIZE : (j + 1) * HEAD_SIZE]
            terms = jnp.exp(score_ref[c] - highest)
            total = total + jnp.sum(terms, axis=-1, keepdims=True)
            mixed = mixed + multiply(terms.astype(jnp.bfloat16), values)
        outs += head_columns(mixed / total, length)
        totals += head_columns(highest + jnp.log(total), length)
    out_ref[...] = jnp.concatenate(outs, axis=1).astype(jnp.bfloat16)
    store_log_totals(lse_ref, totals)


def cross_backward_kernel(chunks, count_ref, base_ref, q_ref, g_ref, lse_ref, *refs):
    k_refs, v_refs = refs[:chunks], refs[chunks : 2 * chunks]
    dq_ref = refs[2 * chunks]
    d_refs = refs[2 * chunks + 1 : 3 * chunks + 1]
    probs_ref, product_ref = refs[3 * chunks + 1 :]
    length, rows = q_ref.shape[0], k_refs[0].shape[1]
    half = d_refs[0].shape[2] // 2
    count = count_ref[pl.program_id(0)]
    first = pl.program_id(1) * (PAIR * HEAD_SIZE)
    position = lax.broadcasted_iota(jnp.int32, (rows, 1), 0)
    dqs = []
    dks, dvs = [[] for _ in range(chunks)], [[] for _ in range(chunks)]
    for j in range(PAIR):
        queries = head_rows(q_ref, j)
        gradient = head_rows(g_ref, j)
        log_total = jnp.concatenate(
            [lse_ref[0, 0, j * SHARED + i : j * SHARED + i + 1, :] for i in range(SHARED)], axis=1
        )
        centre = 0.0
        for c in range(chunks):
            keys = k_refs[c][0, :, j * HEAD_SIZE : (j + 1) * HEAD_SIZE]
            values = v_refs[c][0, :, j * HEAD_SIZE : (j + 1) * HEAD_SIZE]
            scores = jnp.where(
                position + base_ref[c] < count, times_transposed(keys, queries), MASKED
            )
            probs = jnp.exp(scores - log_total)
            product = probs * times_transposed(values, gradient)
            centre = centre + jnp.sum(product, axis=0, keepdims=True)
            dvs[c].append(multiply(probs.astype(jnp.bfloat16), gradient))
            probs_ref[c] = probs
            product_ref[c] = product
        dq = 0.0
        for c in range(chunks):
            keys = k_refs[c][0, :, j * HEAD_SIZE : (j + 1) * HEAD_SIZE]
            score_grad = (product_ref[c] - probs_ref[c] * centre).astype(jnp.bfloat16)
            dks[c].append(multiply(score_grad, queries))
            dq = dq + outer_sum(keys, score_grad)
        dqs += head_columns(jnp.transpose(dq), length)
    dq_ref[...] = jnp.concatenate(dqs, axis=1).astype(jnp.bfloat16)
    for c in range(chunks):
        d_refs[c][0, :, pl.ds(pl.multiple_of(first, 128), 128)] = jnp.concatenate(
            dks[c], axis=1
        ).astype(jnp.bfloat16)
        d_refs[c][0, :, pl.ds(pl.multiple_of(half + first, 128), 128)] = jnp.concatenate(
            dvs[c], axis=1
        ).astype(jnp.bfloat16)


def feed_forward_kernel(
    n_ref, b_ref, wg_ref, wu_ref, wd_ref, hid_ref, gg_ref, gu_ref, y_ref, gn_ref
):
    root = float(np.sqrt(2.0 / np.pi))

    @pl.when(pl.program_id(0) == 0)
    def _():
        y_ref[...] = jnp.zeros_like(y_ref)
        gn_ref[...] = jnp.zeros_like(gn_ref)

    gate = multiply(n_ref[...], wg_ref[...])
    upward = multiply(n_ref[...], wu_ref[...])
    back = times_transposed(b_ref[...], wd_ref[...])
    square = gate * gate
    bend = jnp.tanh(root * gate * (1.0 + 0.044715 * square))
    half_sum = 0.5 * (1.0 + bend)
    activated = gate * half_sum
    slope = half_sum + 0.5 * gate * (1.0 - bend * bend) * (root * (1.0 + 3 * 0.044715 * square))
    hidden = (activated * upward).astype(jnp.bfloat16)
    grad_gate = (back * upward * slope).astype(jnp.bfloat16)
    grad_upward = (back * activated).astype(jnp.bfloat16)
    hid_ref[...] = hidden
    gg_ref[...] = grad_gate
    gu_ref[...] = grad_upward
    y_ref[...] += multiply(hidden, wd_ref[...])
    gn_ref[...] += times_transposed(grad_gate, wg_ref[...]) + times_transposed(
        grad_upward, wu_ref[...]
    )


def shape(dims, dtype):
    return jax.ShapeDtypeStruct(tuple(dims), dtype)


def self_attention(q, k, v, counts, base):
    seqs, length = counts.shape[0], q.shape[0] // counts.shape[0]
    wide, narrow = STEP_HEADS * HEAD_SIZE, PAIR * HEAD_SIZE
    return pl.pallas_call(
        self_forward_kernel,
        out_shape=(shape(q.shape, jnp.bfloat16), shape((seqs, PAIRS, 8, length), jnp.float32)),
        grid_spec=pltpu.PrefetchScalarGridSpec(
            num_scalar_prefetch=1,
            grid=(seqs, PAIRS),
            in_specs=[
                pl.BlockSpec((length, wide), lambda s, p, _: (s, p)),
                pl.BlockSpec((length, narrow), lambda s, p, _: (s, p)),
                pl.BlockSpec((length, narrow), lambda s, p, _: (s, p)),
                pl.BlockSpec((1, STEP_HEADS, length), lambda s, p, _: (p, 0, 0)),
            ],
            out_specs=(
                pl.BlockSpec((length, wide), lambda s, p, _: (s, p)),
                pl.BlockSpec((1, 1, 8, length), lambda s, p, _: (s, p, 0, 0)),
            ),
        ),
        name="self_forward",
    )(counts, q, k, v, base)


def self_attention_back(q, k, v, counts, base, lse, gradient):
    seqs, length = counts.shape[0], q.shape[0] // counts.shape[0]
    wide, narrow = STEP_HEADS * HEAD_SIZE, PAIR * HEAD_SIZE
    return pl.pallas_call(
        self_backward_kernel,
        out_shape=(
            shape(q.shape, jnp.bfloat16),
            shape(k.shape, jnp.bfloat16),
            shape(v.shape, jnp.bfloat16),
            shape((seqs, PAIRS, STEP_HEADS, length), jnp.float32),
        ),
        grid_spec=pltpu.PrefetchScalarGridSpec(
            num_scalar_prefetch=1,
            grid=(seqs, PAIRS),
            in_specs=[
                pl.BlockSpec((length, wide), lambda s, p, _: (s, p)),
                pl.BlockSpec((length, narrow), lambda s, p, _: (s, p)),
                pl.BlockSpec((length, narrow), lambda s, p, _: (s, p)),
                pl.BlockSpec((length, wide), lambda s, p, _: (s, p)),
                pl.BlockSpec((1, 1, 8, length), lambda s, p, _: (s, p, 0, 0)),
                pl.BlockSpec((1, STEP_HEADS, length), lambda s, p, _: (p, 0, 0)),
            ],
            out_specs=(
                pl.BlockSpec((length, wide), lambda s, p, _: (s, p)),
                pl.BlockSpec((length, narrow), lambda s, p, _: (s, p)),
                pl.BlockSpec((length, narrow), lambda s, p, _: (s, p)),
                pl.BlockSpec((1, 1, STEP_HEADS, length), lambda s, p, _: (s, p, 0, 0)),
            ),
        ),
        name="self_backward",
    )(counts, q, k, v, gradient, lse, base)


def chunk_specs(pieces):
    rows, narrow = pieces[0].shape[1], PAIR * HEAD_SIZE
    keys = [pl.BlockSpec((1, rows, narrow), lambda s, p, *_: (s, 0, p)) for _ in pieces]
    values = [pl.BlockSpec((1, rows, narrow), lambda s, p, *_: (s, 0, PAIRS + p)) for _ in pieces]
    return keys + values


def cross_attention(q, pieces, counts, bases):
    seqs, length, rows = counts.shape[0], q.shape[0] // counts.shape[0], pieces[0].shape[1]
    wide = STEP_HEADS * HEAD_SIZE
    return pl.pallas_call(
        functools.partial(cross_forward_kernel, len(pieces)),
        out_shape=(shape(q.shape, jnp.bfloat16), shape((seqs, PAIRS, 8, length), jnp.float32)),
        grid_spec=pltpu.PrefetchScalarGridSpec(
            num_scalar_prefetch=2,
            grid=(seqs, PAIRS),
            in_specs=[pl.BlockSpec((length, wide), lambda s, p, *_: (s, p))] + chunk_specs(pieces),
            out_specs=(
                pl.BlockSpec((length, wide), lambda s, p, *_: (s, p)),
                pl.BlockSpec((1, 1, 8, length), lambda s, p, *_: (s, p, 0, 0)),
            ),
            scratch_shapes=[pltpu.VMEM((len(pieces), SHARED * length, rows), jnp.float32)],
        ),
        name="cross_forward",
    )(counts, bases, q, *pieces, *pieces)


def cross_attention_back(q, pieces, counts, bases, lse, gradient):
    seqs, length, rows = counts.shape[0], q.shape[0] // counts.shape[0], pieces[0].shape[1]
    wide, chunks = STEP_HEADS * HEAD_SIZE, len(pieces)
    return pl.pallas_call(
        functools.partial(cross_backward_kernel, chunks),
        out_shape=(shape(q.shape, jnp.bfloat16),)
        + tuple(shape(piece.shape, jnp.bfloat16) for piece in pieces),
        grid_spec=pltpu.PrefetchScalarGridSpec(
            num_scalar_prefetch=2,
            grid=(seqs, PAIRS),
            in_specs=[
                pl.BlockSpec((length, wide), lambda s, p, *_: (s, p)),
                pl.BlockSpec((length, wide), lambda s, p, *_: (s, p)),
                pl.BlockSpec((1, 1, 8, length), lambda s, p, *_: (s, p, 0, 0)),
            ]
            + chunk_specs(pieces),
            out_specs=(pl.BlockSpec((length, wide), lambda s, p, *_: (s, p)),)
            + tuple(
                pl.BlockSpec((1,) + piece.shape[1:], lambda s, p, *_: (s, 0, 0)) for piece in pieces
            ),
            scratch_shapes=[pltpu.VMEM((chunks, rows, SHARED * length), jnp.float32)] * 2,
        ),
        name="cross_backward",
    )(counts, bases, q, gradient, lse, *pieces, *pieces)


def feed_forward(rows_normed, branch, w_gate, w_up, w_down):
    rows, width = rows_normed.shape
    hidden = w_gate.shape[1]
    tile = 256
    return pl.pallas_call(
        feed_forward_kernel,
        out_shape=(shape((rows, hidden), jnp.bfloat16),) * 3
        + (shape((rows, width), jnp.float32),) * 2,
        grid=(hidden // tile,),
        in_specs=[
            pl.BlockSpec((rows, width), lambda f: (0, 0)),
            pl.BlockSpec((rows, width), lambda f: (0, 0)),
            pl.BlockSpec((width, tile), lambda f: (0, f)),
            pl.BlockSpec((width, tile), lambda f: (0, f)),
            pl.BlockSpec((tile, width), lambda f: (f, 0)),
        ],
        out_specs=(pl.BlockSpec((rows, tile), lambda f: (0, f)),) * 3
        + (pl.BlockSpec((rows, width), lambda f: (0, 0)),) * 2,
        name="feed_forward",
    )(rows_normed, branch, w_gate, w_up, w_down)


def bit_count(size):
    return size.bit_length() - 1


def reduce_rows(term, order):
    devices, members = lax.axis_size("dp"), lax.axis_size("mem")
    me, member = lax.axis_index("dp"), lax.axis_index("mem")
    bits = bit_count(devices)
    rows, columns = term.shape
    share = rows // (devices * members)
    current = term.reshape((2,) * bits + (members, share, columns))
    left = list(range(bits - 1, -1, -1))
    for bit in order:
        axis = left.index(bit)
        left.remove(bit)
        mine = (me >> bit) & 1
        sent = lax.dynamic_index_in_dim(current, 1 - mine, axis, keepdims=False)
        got = lax.ppermute(sent, "dp", [(i, i ^ (1 << bit)) for i in range(devices)])
        kept = lax.dynamic_index_in_dim(current, mine, axis, keepdims=False)
        current = (kept.astype(jnp.float32) + got.astype(jnp.float32)).astype(jnp.bfloat16)
    total = lax.dynamic_index_in_dim(current, member, 0, keepdims=False).astype(jnp.float32)
    for sign in (1, -1):
        got = None
        for step in range(members - 1):
            place = member if sign == 1 else members - 1 - member
            block = jnp.clip(members - 1 - step + place, 0, members - 1)
            block = block if sign == 1 else members - 1 - block
            sent = lax.dynamic_index_in_dim(current, block, 0, keepdims=False)
            if got is not None:
                sent = (sent.astype(jnp.float32) + got.astype(jnp.float32)).astype(jnp.bfloat16)
            pairs = [(i, i + 1) for i in range(step + 1)]
            if sign == -1:
                pairs = [(members - 1 - a, members - 1 - b) for a, b in pairs]
            got = lax.ppermute(sent, "mem", pairs)
        total = total + got.astype(jnp.float32)
    return total


LANES = 128


def partner_masks(order):
    stages = len(order)
    masks = []
    for place in range(1 << stages):
        mask = 0
        for stage, bit in enumerate(order):
            if not (place >> (stages - 1 - stage)) & 1:
                mask |= 1 << bit
        masks.append(mask)
    return masks


def outer_kernel(lefts, chunk, segments, orders, me_ref, *refs):
    a_refs, refs = refs[:lefts], refs[lefts:]
    b_refs, refs = refs[: lefts * len(segments)], refs[lefts * len(segments) :]
    outs, refs = refs[: 2 * len(orders)], refs[2 * len(orders) :]
    plain_ref, arranged = refs[0], refs[1:]
    blocks = 1 << len(orders[0])
    block = plain_ref.shape[0] // blocks
    members, share = outs[0].shape[1], outs[0].shape[2] // chunk
    me = me_ref[0]

    @pl.when(pl.program_id(0) == 0)
    def _():
        tokens = a_refs[0].shape[0]
        for index, a_ref in enumerate(a_refs):
            plain_ref[:, index * tokens : (index + 1) * tokens] = jnp.transpose(a_ref[...])
        for order, arranged_ref in zip(orders, arranged):
            for place, mask in enumerate(partner_masks(order)):
                source = pl.multiple_of((me ^ mask) * block, 16)
                arranged_ref[place * block : (place + 1) * block] = plain_ref[
                    pl.ds(source, block)
                ]

    step = 0
    for index, (steps, color) in enumerate(segments):
        rights = b_refs[lefts * index : lefts * (index + 1)]

        @pl.when((pl.program_id(0) >= step) & (pl.program_id(0) < step + steps))
        def _(color=color, rights=rights):
            right = joined([right_ref[...] for right_ref in rights], 0)
            product = multiply(arranged[color][...], right).astype(jnp.bfloat16)
            for place in range(blocks):
                half_ref = outs[2 * color + (0 if place < blocks // 2 else 1)]
                for m in range(members):
                    first = place * block + m * share
                    for tile in range(chunk):
                        half_ref[place % (blocks // 2), m, tile * share : (tile + 1) * share] = (
                            product[first : first + share, tile * LANES : (tile + 1) * LANES]
                        )

        step += steps


def outer_arranged(lefts, parts, orders, chunk):
    tokens, features = lefts[0].shape
    devices, members = lax.axis_size("dp"), lax.axis_size("mem")
    share = features // (devices * members)
    half = devices // 2
    wide = chunk * LANES
    segments, in_specs, operands, step = [], [], [], 0
    totals = [0] * len(orders)
    for rights, first, columns, color in parts:
        steps = columns // wide
        segments.append((steps, color))
        totals[color] += steps
        for right in rights:
            operands.append(right)
            in_specs.append(
                pl.BlockSpec(
                    (tokens, wide),
                    lambda j, _, step=step, steps=steps, first=first: (
                        0,
                        first // wide + jnp.clip(j - step, 0, steps - 1),
                    ),
                )
            )
        step += steps
    out_shape, out_specs, before = [], [], 0
    for total in totals:
        for _ in range(2):
            out_shape.append(shape((half, members, share * chunk * total, LANES), jnp.bfloat16))
            out_specs.append(
                pl.BlockSpec(
                    (half, members, share * chunk, LANES),
                    lambda j, _, before=before, total=total: (
                        0,
                        0,
                        jnp.clip(j - before, 0, total - 1),
                        0,
                    ),
                )
            )
        before += total
    me = lax.axis_index("dp").astype(jnp.int32).reshape(1)
    kernel = functools.partial(
        outer_kernel, len(lefts), chunk, tuple(segments), tuple(tuple(o) for o in orders)
    )
    return pl.pallas_call(
        kernel,
        out_shape=tuple(out_shape),
        grid_spec=pltpu.PrefetchScalarGridSpec(
            num_scalar_prefetch=1,
            grid=(step,),
            in_specs=[pl.BlockSpec((tokens, features), lambda j, _: (0, 0))] * len(lefts) + in_specs,
            out_specs=tuple(out_specs),
            scratch_shapes=[pltpu.VMEM((features, tokens * len(lefts)), jnp.bfloat16)]
            * (1 + len(orders)),
        ),
        name="outer",
    )(me, *lefts, *operands)


def project_kernel(members, place_ref, x_ref, ck_ref, cv_ref, *out_refs):
    width = ck_ref.shape[1]
    for index in range(members):

        @pl.when(pl.program_id(0) == index)
        def _(index=index):
            out_ref = out_refs[index]
            rows = x_ref[0].reshape(-1, x_ref.shape[-1])
            kept = out_ref.shape[:2] + (width,)
            out_ref[:, :, :width] = (
                multiply(rows, ck_ref[...]).astype(jnp.bfloat16).reshape(kept)
            )
            out_ref[:, :, width:] = (
                multiply(rows, cv_ref[...]).astype(jnp.bfloat16).reshape(kept)
            )


def project_memory(memory, m, seqs, c_key, c_value):
    members = lax.axis_size("mem")
    _, _, rows, width = memory.shape
    kept = (seqs, rows, c_key.shape[1] + c_value.shape[1])
    me = lax.axis_index("mem").astype(jnp.int32).reshape(1)
    found = pl.pallas_call(
        functools.partial(project_kernel, members),
        out_shape=(shape(kept, jnp.bfloat16),) * members,
        grid_spec=pltpu.PrefetchScalarGridSpec(
            num_scalar_prefetch=1,
            grid=(members,),
            in_specs=[
                pl.BlockSpec(
                    (1, seqs, rows, width),
                    lambda t, me: (m, lax.rem(me[0] + t + 1, members), 0, 0),
                ),
                pl.BlockSpec(c_key.shape, lambda t, _: (0, 0)),
                pl.BlockSpec(c_value.shape, lambda t, _: (0, 0)),
            ],
            out_specs=(pl.BlockSpec(kept, lambda t, _: (0, 0, 0)),) * members,
        ),
        name="project",
    )(me, memory, c_key, c_value)
    return [found[-1]] + list(found[:-1])


def memory_kernel(pieces, orders, place_ref, x_ref, ck_ref, cv_ref, *refs):
    piece_refs, refs = refs[:pieces], refs[pieces:]
    grad_ref, outs, (now_ref, sum_ref) = refs[0], refs[1:5], refs[5:]
    step, width = pl.program_id(0), ck_ref.shape[1]

    @pl.when(step == 0)
    def _():
        sum_ref[...] = jnp.zeros_like(sum_ref)

    for index in range(pieces):

        @pl.when(step == index)
        def _(index=index):
            now_ref[...] = piece_refs[index][...].reshape(now_ref.shape)

    now = now_ref[...]
    grad = times_transposed(now[:, :width], ck_ref[...]) + times_transposed(
        now[:, width:], cv_ref[...]
    )
    grad_ref[0] = grad.astype(jnp.bfloat16).reshape(grad_ref.shape[1:])
    sum_ref[...] += outer_sum(x_ref[0].reshape(-1, x_ref.shape[-1]), now)

    @pl.when(step == pieces - 1)
    def _():
        blocks = 1 << len(orders[0])
        block = sum_ref.shape[0] // blocks
        members = outs[0].shape[1]
        tiles = width // LANES
        share = block // members
        for color, order in enumerate(orders):
            for place, mask in enumerate(partner_masks(order)):
                source = pl.multiple_of((place_ref[0] ^ mask) * block, 8)
                half_ref = outs[2 * color + (0 if place < blocks // 2 else 1)]
                found = sum_ref[pl.ds(source, block), color * width : (color + 1) * width]
                found = found.astype(jnp.bfloat16)
                for m in range(members):
                    for tile in range(tiles):
                        half_ref[place % (blocks // 2), m, tile * share : (tile + 1) * share] = (
                            found[m * share : (m + 1) * share, tile * LANES : (tile + 1) * LANES]
                        )


def memory_backward(memory, pieces, c_key, c_value, orders):
    devices, members = lax.axis_size("dp"), lax.axis_size("mem")
    seqs, rows, both = pieces[0].shape
    width = memory.shape[-1]
    half, share = devices // 2, width // (devices * members)
    kept = (half, members, share * (both // 2 // LANES), LANES)
    place = jnp.stack([lax.axis_index("dp"), lax.axis_index("mem")]).astype(jnp.int32)

    def block_index(t, place):
        return (t // members, lax.rem(place[1] + lax.rem(t, members), members), 0, 0)

    found = pl.pallas_call(
        functools.partial(memory_kernel, len(pieces), tuple(tuple(o) for o in orders)),
        out_shape=(shape(memory.shape, jnp.bfloat16),) + (shape(kept, jnp.bfloat16),) * 4,
        grid_spec=pltpu.PrefetchScalarGridSpec(
            num_scalar_prefetch=1,
            grid=(len(pieces),),
            in_specs=[
                pl.BlockSpec((1, seqs, rows, width), block_index),
                pl.BlockSpec(c_key.shape, lambda t, _: (0, 0)),
                pl.BlockSpec(c_value.shape, lambda t, _: (0, 0)),
            ]
            + [pl.BlockSpec((seqs, rows, both), lambda t, _: (0, 0, 0))] * len(pieces),
            out_specs=(pl.BlockSpec((1, seqs, rows, width), block_index),)
            + (pl.BlockSpec(kept, lambda t, _: (0, 0, 0, 0)),) * 4,
            scratch_shapes=[
                pltpu.VMEM((seqs * rows, both), jnp.bfloat16),
                pltpu.VMEM((width, both), jnp.float32),
            ],
        ),
        name="memory_backward",
    )(place, memory, c_key, c_value, *pieces)
    return found[0], found[1:3], found[3:5]


def swap(array, bit):
    size = lax.axis_size("dp")
    return lax.ppermute(array, "dp", [(i, i ^ (1 << bit)) for i in range(size)])


def add16(left, right):
    return (left.astype(jnp.float32) + right.astype(jnp.float32)).astype(jnp.bfloat16)


def joined(arrays, axis):
    return arrays[0] if len(arrays) == 1 else jnp.concatenate(arrays, axis=axis)


def first_swap(pairs, bit):
    return [(swap(sent, bit), kept) for sent, kept in pairs]


def halves_of(pairs):
    half = pairs[0][0].shape[0] // 2
    sent = joined([add16(kept[:half], got[:half]) for got, kept in pairs], 2)
    kept = joined([add16(kept[half:], got[half:]) for got, kept in pairs], 2)
    return sent, kept


def next_stage(pairs, bit):
    sent, kept = halves_of(pairs)
    return [(swap(sent, bit), kept)]


def later_stages(pairs, bits):
    for bit in bits:
        pairs = next_stage(pairs, bit)
    return pairs


def whole_of(pairs):
    return joined([add16(kept, got) for got, kept in pairs], 2)[0]


def along_members(current):
    members, member = lax.axis_size("mem"), lax.axis_index("mem")
    total = lax.dynamic_index_in_dim(current, member, 0, keepdims=False).astype(jnp.float32)
    got = [None, None]
    for step in range(members - 1):
        for side in range(2):
            place = member if side == 0 else members - 1 - member
            block = jnp.clip(members - 1 - step + place, 0, members - 1)
            block = block if side == 0 else members - 1 - block
            sent = lax.dynamic_index_in_dim(current, block, 0, keepdims=False)
            if step:
                sent = add16(sent, got[side])
            pairs = [(i, i + 1) for i in range(step + 1)]
            if side == 1:
                pairs = [(members - 1 - a, members - 1 - b) for a, b in pairs]
            got[side] = lax.ppermute(sent, "mem", pairs)
    return total + got[0].astype(jnp.float32) + got[1].astype(jnp.float32)


def members_sum(pairs):
    flat = [item for pair in pairs for item in pair if item is not None]
    ends = np.cumsum([0] + [item.shape[1] for item in flat])
    total = along_members(jnp.concatenate(flat, axis=1))
    parts = iter([total[ends[i] : ends[i + 1]] for i in range(len(flat))])
    return [tuple(None if item is None else next(parts) for item in pair) for pair in pairs]


def rows_out(total, share, columns, first):
    tiles = columns // LANES
    part = total[first : first + share * tiles].reshape(tiles, share, LANES)
    return part.transpose(1, 0, 2).reshape(share, columns)


def sum_everywhere(value):
    for axis in ("mem", "dp"):
        size = lax.axis_size(axis)
        for bit in range(bit_count(size)):
            value = value + lax.ppermute(value, axis, [(i, i ^ (1 << bit)) for i in range(size)])
    return value


def per_device(
    target_in,
    memory,
    target_len,
    mem_len,
    cotangent,
    gain_self,
    gain_cross,
    gain_ffn,
    rel_table,
    w_query,
    w_key,
    w_value,
    w_out,
    c_query,
    c_key,
    c_value,
    c_out,
    w_gate,
    w_up,
    w_down,
):
    micro, seqs, length, width = target_in.shape
    mem_rows = memory.shape[2]
    members, member = lax.axis_size("mem"), lax.axis_index("mem")
    devices = lax.axis_size("dp")
    bits = bit_count(devices)
    order_a = list(range(bits))
    order_b = [0] + order_a[:0:-1]
    orders = (order_a, order_b)
    count, rows = micro * seqs, seqs * length
    key_width, hidden_width = c_key.shape[1], w_gate.shape[1]
    share, share_down = width // (devices * members), hidden_width // (devices * members)
    half = width // 2
    steps = range(micro)

    def shifted(array, shift):
        return lax.ppermute(array, "mem", [(i, (i + shift) % members) for i in range(members)])

    pieces = []
    for m in steps:
        found = project_memory(memory, m, seqs, c_key, c_value)
        pieces.append([found[0]] + [shifted(found[i], i) for i in range(1, members)])
    bases = jnp.stack(
        [lax.rem(member + members - shift, members) * mem_rows for shift in range(members)]
    ).astype(jnp.int32)

    target_counts = target_len.reshape(count)
    onehot = bucket_onehot(length)
    backwards = onehot[:, (-np.arange(length)) % length]
    base = jnp.dot(rel_table.T, jnp.asarray(onehot), precision=EXACT_PRECISION)
    base = base.reshape(PAIRS, STEP_HEADS, length)
    base_back = jnp.dot(rel_table.T, jnp.asarray(backwards), precision=EXACT_PRECISION)
    base_back = base_back.reshape(PAIRS, STEP_HEADS, length)

    inputs = target_in.reshape(count * length, width).astype(jnp.float32)
    normed_self = normed(inputs, gain_self)
    queries = multiply(normed_self, w_query).astype(jnp.bfloat16)
    keys = multiply(normed_self, w_key).astype(jnp.bfloat16)
    values = multiply(normed_self, w_value).astype(jnp.bfloat16)
    attended, self_lse = self_attention(queries, keys, values, target_counts, base_back)

    position = jnp.arange(length)
    outs, after_selfs, normed_crosses, cross_queries_all, mixed_all = [], [], [], [], []
    normed_ffns, branches_ffn, hiddens, gates, ups = [], [], [], [], []
    branches_cross, grad_queries_cross, branches_self = [], [], []
    grad_after_selfs, grads_attended = [], []
    sum_gain_ffn = sum_gain_cross = 0.0
    for m in steps:
        after_self = inputs[m * rows : (m + 1) * rows] + multiply(
            attended[m * rows : (m + 1) * rows], w_out
        )
        after_selfs.append(after_self)
        normed_crosses.append(normed(after_self, gain_cross))
        cross_queries_all.append(multiply(normed_crosses[m], c_query).astype(jnp.bfloat16))
    grad_pieces = []
    for m in steps:
        after_self, cross_queries = after_selfs[m], cross_queries_all[m]
        memory_counts = mem_len[m]
        cross_mixed, cross_lse = cross_attention(cross_queries, pieces[m], memory_counts, bases)
        mixed_all.append(cross_mixed)
        after_cross = after_self + multiply(cross_mixed, c_out)
        normed_ffn = normed(after_cross, gain_ffn)
        normed_ffns.append(normed_ffn)
        valid = (position[None, :] < target_len[m][:, None]).reshape(rows, 1)
        branch_ffn = jnp.where(valid, cotangent[m].reshape(rows, width), 0)
        branches_ffn.append(branch_ffn)
        grad_result = branch_ffn.astype(jnp.float32)
        hidden, grad_gate, grad_upward, ffn_out, grad_normed = feed_forward(
            normed_ffn, branch_ffn, w_gate, w_up, w_down
        )
        hiddens.append(hidden)
        gates.append(grad_gate)
        ups.append(grad_upward)
        outs.append(jnp.where(valid, after_cross + ffn_out, 0.0).astype(jnp.bfloat16))
        if m == micro - 1:
            gate_pairs = []
            for rights, order in ((gates, order_a), (ups, order_b)):
                found = outer_arranged(
                    normed_ffns,
                    [(rights, 0, hidden_width, 0)],
                    (order,),
                    hidden_width // (2 * LANES),
                )
                found = first_swap([found], 0)
                gate_pairs.append(next_stage(found, order[1]))
            packed_down = share_down % 8 == 0 and (hidden_width // devices) % 16 == 0
            if packed_down:
                found = outer_arranged(
                    hiddens,
                    [(branches_ffn, 0, half, 0), (branches_ffn, half, half, 1)],
                    orders,
                    half // LANES,
                )
                down_pairs = first_swap([found[0:2]], 0), first_swap([found[2:4]], 0)
                down_pairs = [
                    next_stage(pairs, order[1]) for pairs, order in zip(down_pairs, orders)
                ]
        part, gain_part = norm_back(after_cross, gain_ffn, grad_normed)
        sum_gain_ffn = sum_gain_ffn + gain_part
        grad_after_cross = grad_result + part
        branch_cross = grad_after_cross.astype(jnp.bfloat16)
        branches_cross.append(branch_cross)
        grad_cross_mixed = times_transposed(branch_cross, c_out).astype(jnp.bfloat16)
        found = cross_attention_back(
            cross_queries, pieces[m], memory_counts, bases, cross_lse, grad_cross_mixed
        )
        grad_queries_cross.append(found[0])
        for shift in range(members):
            piece = found[1 + shift]
            if shift:
                piece = shifted(piece, members - shift)
            grad_pieces.append(piece)
        part, gain_part = norm_back(
            after_self, gain_cross, times_transposed(found[0], c_query)
        )
        sum_gain_cross = sum_gain_cross + gain_part
        grad_after_self = grad_after_cross + part
        grad_after_selfs.append(grad_after_self)
        branches_self.append(grad_after_self.astype(jnp.bfloat16))
        grads_attended.append(times_transposed(branches_self[m], w_out).astype(jnp.bfloat16))
    chunk = key_width // LANES
    c_out_sum = outer_arranged(mixed_all, [(branches_cross, 0, width, 0)], (order_a,), chunk)
    c_query_sum = outer_arranged(
        normed_crosses, [(grad_queries_cross, 0, width, 0)], (order_b,), chunk
    )
    attended_parts = [attended[m * rows : (m + 1) * rows] for m in steps]
    w_out_sum = outer_arranged(
        attended_parts,
        [(branches_self, 0, half, 0), (branches_self, half, half, 1)],
        orders,
        chunk,
    )
    rest_pairs = (
        first_swap([c_out_sum, w_out_sum[0:2]], 0),
        first_swap([c_query_sum, w_out_sum[2:4]], 0),
    )
    ffn = [[whole_of(later_stages(p, o[2:])) for p, o in zip(gate_pairs, orders)]]
    if packed_down:
        ffn.append([whole_of(later_stages(p, o[2:])) for p, o in zip(down_pairs, orders)])
    rest_pairs = [next_stage(p, o[1]) for p, o in zip(rest_pairs, orders)]
    rest_a, rest_b = [whole_of(later_stages(p, o[2:])) for p, o in zip(rest_pairs, orders)]

    grad_queries, grad_keys, grad_values, diagonals = self_attention_back(
        queries,
        keys,
        values,
        target_counts,
        base,
        self_lse,
        jnp.concatenate(grads_attended, axis=0),
    )
    w_self_sum = outer_arranged(
        [normed_self],
        [
            ([grad_keys], 0, key_width, 0),
            ([grad_queries], 0, width, 1),
            ([grad_values], 0, key_width, 1),
        ],
        orders,
        chunk,
    )
    self_pairs = first_swap([w_self_sum[0:2]], 0), first_swap([w_self_sum[2:4]], 0)
    self_pairs = [next_stage(p, o[1]) for p, o in zip(self_pairs, orders)]
    self_a, self_b = [whole_of(later_stages(p, o[2:])) for p, o in zip(self_pairs, orders)]
    (gate_a, gate_b), (down_a, down_b) = members_sum(ffn + [(None, None)] * (2 - len(ffn)))
    g_gate = rows_out(gate_a, share, hidden_width, 0)
    g_up = rows_out(gate_b, share, hidden_width, 0)
    if packed_down:
        g_down = jnp.concatenate(
            [rows_out(part, share_down, half, 0) for part in (down_a, down_b)], axis=1
        )
    else:
        g_down = reduce_rows(
            outer_sum(jnp.concatenate(hiddens), jnp.concatenate(branches_ffn)).astype(jnp.bfloat16),
            order_a,
        )

    grad_normed = (
        times_transposed(grad_queries, w_query)
        + times_transposed(grad_keys, w_key)
        + times_transposed(grad_values, w_value)
    )
    part, sum_gain_self = norm_back(inputs, gain_self, grad_normed)
    target_grad = (jnp.concatenate(grad_after_selfs, axis=0) + part).astype(jnp.bfloat16)
    distances = jnp.sum(diagonals, axis=0).reshape(QUERY_HEADS, length)
    table = jnp.dot(distances, jnp.asarray(onehot.T), precision=EXACT_PRECISION).T

    memory_grad, memory_a, memory_b = memory_backward(memory, grad_pieces, c_key, c_value, orders)
    pairs_a = first_swap([memory_a], 0)
    pairs_b = first_swap([memory_b], 0)
    memory_a = whole_of(later_stages(pairs_a, order_a[1:]))
    memory_b = whole_of(later_stages(pairs_b, order_b[1:]))
    (rest_a, rest_b), (self_a, self_b), (memory_a, memory_b) = members_sum(
        [(rest_a, rest_b), (self_a, self_b), (memory_a, memory_b)]
    )
    tile_rows = share * (width // LANES)
    g_c_out = rows_out(rest_a, share, width, 0)
    g_c_query = rows_out(rest_b, share, width, 0)
    g_w_out = jnp.concatenate(
        [rows_out(part, share, half, tile_rows) for part in (rest_a, rest_b)], axis=1
    )
    g_w_key = rows_out(self_a, share, key_width, 0)
    g_w_query = rows_out(self_b, share, width, 0)
    g_w_value = rows_out(self_b, share, key_width, tile_rows)
    g_c_key = rows_out(memory_a, share, key_width, 0)
    g_c_value = rows_out(memory_b, share, key_width, 0)

    small = sum_everywhere(
        jnp.concatenate([sum_gain_self, sum_gain_cross, sum_gain_ffn, table.reshape(-1)])
    )
    return (
        jnp.stack(outs).reshape(micro, seqs, length, width),
        target_grad.reshape(micro, seqs, length, width),
        memory_grad,
        small[:width],
        small[width : 2 * width],
        small[2 * width : 3 * width],
        small[3 * width :].reshape(NB, QUERY_HEADS),
        g_w_query,
        g_w_key,
        g_w_value,
        g_w_out,
        g_c_query,
        g_c_key,
        g_c_value,
        g_c_out,
        g_gate,
        g_up,
        g_down,
    )


def solution(mesh):
    rows = P(None, ("dp", "mem"), None, None)
    lengths = P(None, ("dp", "mem"))
    encoded = P(None, "dp", "mem", None)
    return jax.shard_map(
        per_device,
        mesh=mesh,
        in_specs=(rows, encoded, lengths, lengths, rows) + (P(),) * 15,
        out_specs=(rows, rows, encoded) + (P(),) * 4 + (P(("dp", "mem"), None),) * 11,
        check_vma=False,
    )
```

profile of v0, /device:TPU:0, one launch (start us, length us, event | category | flops | bytes accessed | tf_op | source)
XLA Modules:
  0.0 582.6 jit_solution(13577001304128651318)
XLA Ops:
  0.7 6.6 %project.2 = (bf16[1,256,1024]{2,1,0:T(8,128)(2,1)}, bf16[1,256,1024]{2,1,0:T(8,128)(2,1)}, bf16[1,256,1024]{2,1,0:T(8,128)(2,1)}, bf16[1,256,1024]{2,1,0:T(8,128)(2,1)}) custom-call(s32[1]{0:T(128)} %bitcast.10.place_ref, bf16[2,4,256,1024]{3,2,1,0:T(8,128)(2,1)} %x_ref.5, bf16[1024,512]{1,0:T(8,128)(2,1)} %ck_ref.5, bf16[1024,512]{1,0:T(8,128)(2,1)} %cv_ref.5), custom_call_target="tpu_custom_call" | custom-call | tf_op jit(solution)/shard_map/project/pallas_call | solution.py:608
  14.2 6.4 %project.3 = (bf16[1,256,1024]{2,1,0:T(8,128)(2,1)}, bf16[1,256,1024]{2,1,0:T(8,128)(2,1)}, bf16[1,256,1024]{2,1,0:T(8,128)(2,1)}, bf16[1,256,1024]{2,1,0:T(8,128)(2,1)}) custom-call(s32[1]{0:T(128)} %bitcast.10.place_ref, bf16[2,4,256,1024]{3,2,1,0:T(8,128)(2,1)} %x_ref.5, bf16[1024,512]{1,0:T(8,128)(2,1)} %ck_ref.5, bf16[1024,512]{1,0:T(8,128)(2,1)} %cv_ref.5), custom_call_target="tpu_custom_call" | custom-call | tf_op jit(solution)/shard_map/project/pallas_call | solution.py:608
  31.1 14.6 %self_forward.1 = (bf16[512,1024]{1,0:T(8,128)(2,1)}, f32[2,4,8,256]{3,2,1,0:T(8,128)}) custom-call(s32[2]{0:T(128)} %bitcast.292, bf16[512,1024]{1,0:T(8,128)(2,1)} %convolution_convert_fusion.q_ref, bf16[512,512]{1,0:T(8,128)(2,1)} %convolution_convert_fusion.8.k_ref, bf16[512,512]{1,0:T(8,128)(2,1)} %convolution_convert_fusion.7.v_ref, ...), custom_call_target="tpu_custom_call" | custom-call | tf_op jit(solution)/shard_map/self_forward/pallas_call | solution.py:303
  63.1 12.2 %cross_forward.2 = (bf16[256,1024]{1,0:T(8,128)(2,1)}, f32[1,4,8,256]{3,2,1,0:T(8,128)}) custom-call(s32[1]{0:T(128)} %bitcast.5.count_ref, s32[4]{0:T(128)} %pad_add_fusion.base_ref, bf16[256,1024]{1,0:T(8,128)(2,1)} %convolution_convert_fusion.6.q_ref, bf16[1,256,1024]{2,1,0:T(8,128)(2,1)} %get-tuple-element.82.refs_0_.refs_4_, ...), custom_call_target="tpu_custom_call" | custom-call | tf_op jit(solution)/shard_map/cross_forward/pallas_call | solution.py:367
  80.0 17.3 %feed_forward.2 = (bf16[256,2816]{1,0:T(8,128)(2,1)}, bf16[256,2816]{1,0:T(8,128)(2,1)}, bf16[256,2816]{1,0:T(8,128)(2,1)}, f32[256,1024]{1,0:T(8,128)}, f32[256,1024]{1,0:T(8,128)}) custom-call(bf16[256,1024]{1,0:T(8,128)(2,1)} %multiply_convert_fusion.2.n_ref.refs_0_, bf16[256,1024]{1,0:T(8,128)(2,1)} %get-tuple-element.234.b_ref.refs_2_.refs_4_, ...), custom_call_target="tpu_custom_call" | custom-call | tf_op jit(solution)/shard_map/feed_forward/pallas_call | solution.py:414
  102.7 17.1 %cross_backward.2 = (bf16[256,1024]{1,0:T(8,128)(2,1)}, bf16[1,256,1024]{2,1,0:T(8,128)(2,1)}, bf16[1,256,1024]{2,1,0:T(8,128)(2,1)}, bf16[1,256,1024]{2,1,0:T(8,128)(2,1)}, bf16[1,256,1024]{2,1,0:T(8,128)(2,1)}) custom-call(s32[1]{0:T(128)} %bitcast.5.count_ref, s32[4]{0:T(128)} %pad_add_fusion.base_ref, bf16[256,1024]{1,0:T(8,128)(2,1)} %convolution_convert_fusion.6.q_ref, ...), custom_call_target="tpu_custom_call" | custom-call | tf_op jit(solution)/shard_map/cross_backward/pallas_call | solution.py:387
  125.5 12.4 %cross_forward.3 = (bf16[256,1024]{1,0:T(8,128)(2,1)}, f32[1,4,8,256]{3,2,1,0:T(8,128)}) custom-call(s32[1]{0:T(128)} %bitcast.15.count_ref, s32[4]{0:T(128)} %pad_add_fusion.base_ref, bf16[256,1024]{1,0:T(8,128)(2,1)} %convolution_convert_fusion.5.q_ref, bf16[1,256,1024]{2,1,0:T(8,128)(2,1)} %get-tuple-element.88.refs_0_.refs_4_, ...), custom_call_target="tpu_custom_call" | custom-call | tf_op jit(solution)/shard_map/cross_forward/pallas_call | solution.py:367
  144.3 17.3 %feed_forward.3 = (bf16[256,2816]{1,0:T(8,128)(2,1)}, bf16[256,2816]{1,0:T(8,128)(2,1)}, bf16[256,2816]{1,0:T(8,128)(2,1)}, f32[256,1024]{1,0:T(8,128)}, f32[256,1024]{1,0:T(8,128)}) custom-call(bf16[256,1024]{1,0:T(8,128)(2,1)} %get-tuple-element.248.n_ref.refs_1_, bf16[256,1024]{1,0:T(8,128)(2,1)} %get-tuple-element.235.b_ref.refs_3_.refs_5_, ...), custom_call_target="tpu_custom_call" | custom-call | tf_op jit(solution)/shard_map/feed_forward/pallas_call | solution.py:414
  167.1 17.2 %cross_backward.3 = (bf16[256,1024]{1,0:T(8,128)(2,1)}, bf16[1,256,1024]{2,1,0:T(8,128)(2,1)}, bf16[1,256,1024]{2,1,0:T(8,128)(2,1)}, bf16[1,256,1024]{2,1,0:T(8,128)(2,1)}, bf16[1,256,1024]{2,1,0:T(8,128)(2,1)}) custom-call(s32[1]{0:T(128)} %bitcast.15.count_ref, s32[4]{0:T(128)} %pad_add_fusion.base_ref, ...), custom_call_target="tpu_custom_call" | custom-call | tf_op jit(solution)/shard_map/cross_backward/pallas_call | solution.py:387
  191.4 12.1 %self_backward.1 = (bf16[512,1024]{1,0:T(8,128)(2,1)}, bf16[512,512]{1,0:T(8,128)(2,1)}, bf16[512,512]{1,0:T(8,128)(2,1)}, f32[2,4,4,256]{3,2,1,0:T(4,128)}) custom-call(s32[2]{0:T(128)} %bitcast.293, bf16[512,1024]{1,0:T(8,128)(2,1)} %convolution_convert_fusion.q_ref, bf16[512,512]{1,0:T(8,128)(2,1)} %convolution_convert_fusion.8.k_ref, ...), custom_call_target="tpu_custom_call" | custom-call | tf_op jit(solution)/shard_map/self_backward/pallas_call | solution.py:327
  203.5 4.6 fusion.58
  210.8 4.9 fusion.7
  215.7 18.4 %collective-permute-start.12 = (f32[3584]{0:T(1024)S(1)}, f32[3584]{0:T(1024)S(1)}, u32[]{:S(2)}, u32[]{:S(2)}) collective-permute-start(f32[3584]{0:T(1024)S(1)} %pad_maximum_fusion.8), channel_id=1, source_target_pairs={{0,1},{1,0},{2,3},{3,2},{4,5},{5,4},{6,7},{7,6},{8,9},{9,8},{10,11... | collective-permute-start | bytes 43016 | tf_op jit(solution)/shard_map/ppermute | solution.py:782
  238.7 9.5 %collective-permute-done.13 = f32[3584]{0:T(1024)S(1)} collective-permute-done((f32[3584]{0:T(1024)S(1)}, f32[3584]{0:T(1024)S(1)}, u32[]{:S(2)}, u32[]{:S(2)}) %collective-permute-start.13) | collective-permute-done | bytes 14368 | tf_op jit(solution)/shard_map/ppermute | solution.py:782
  253.8 6.8 %outer.10 = (bf16[4,4,128,128]{3,2,1,0:T(8,128)(2,1)}, bf16[4,4,128,128]{3,2,1,0:T(8,128)(2,1)}, bf16[4,4,384,128]{3,2,1,0:T(8,128)(2,1)}, bf16[4,4,384,128]{3,2,1,0:T(8,128)(2,1)}) custom-call(s32[1]{0:T(128)} %bitcast.23.me_ref, bf16[512,1024]{1,0:T(8,128)(2,1)} %copy-done.28, bf16[512,512]{1,0:T(8,128)(2,1)} %get-tuple-element.102.refs_1_, ...), custom_call_target="tpu_custom_call" | custom-call | tf_op jit(solution)/shard_map/outer/pallas_call | solution.py:571
  261.7 4.8 outer.8
  271.8 14.9 %collective-permute-done.7.refs_2_ = bf16[1,256,1024]{2,1,0:T(8,128)(2,1)S(1)} collective-permute-done((bf16[1,256,1024]{2,1,0:T(8,128)(2,1)}, bf16[1,256,1024]{2,1,0:T(8,128)(2,1)S(1)}, u32[]{:S(2)}, u32[]{:S(2)}) %collective-permute-start.7) | collective-permute-done | bytes 524320 | tf_op jit(solution)/shard_map/ppermute | solution.py:823
  286.7 21.8 %collective-permute-start.11 = (bf16[1,256,1024]{2,1,0:T(8,128)(2,1)}, bf16[1,256,1024]{2,1,0:T(8,128)(2,1)}, u32[]{:S(2)}, u32[]{:S(2)}) collective-permute-start(bf16[1,256,1024]{2,1,0:T(8,128)(2,1)} %get-tuple-element.111), channel_id=1, source_target_pairs={{0,1},{1,2},{2,3},{3,0},{4,5},{5,6},{6,7},{7,4},{8,9},{9,10},{10,1... | collective-permute-start | bytes 1572872 | tf_op jit(solution)/shard_map/ppermute | solution.py:823
  309.1 4.7 outer.9
  313.8 9.2 %outer.13 = (bf16[4,4,352,128]{3,2,1,0:T(8,128)(2,1)}, bf16[4,4,352,128]{3,2,1,0:T(8,128)(2,1)}, bf16[4,4,352,128]{3,2,1,0:T(8,128)(2,1)}, bf16[4,4,352,128]{3,2,1,0:T(8,128)(2,1)}) custom-call(s32[1]{0:T(128)} %bitcast.23.me_ref, bf16[256,2816]{1,0:T(8,128)(2,1)} %get-tuple-element.138.refs_0_, bf16[256,2816]{1,0:T(8,128)(2,1)} %get-tuple-element.139.refs_1_, ...), custom_call_target="tpu_custom_call" | custom-call | tf_op jit(solution)/shard_map/outer/pallas_call | solution.py:571
  323.0 7.3 %outer.12 = (bf16[4,4,704,128]{3,2,1,0:T(8,128)(2,1)}, bf16[4,4,704,128]{3,2,1,0:T(8,128)(2,1)}) custom-call(s32[1]{0:T(128)} %bitcast.23.me_ref, bf16[256,1024]{1,0:T(8,128)(2,1)} %multiply_convert_fusion.2.n_ref.refs_0_, bf16[256,1024]{1,0:T(8,128)(2,1)} %get-tuple-element.248.n_ref.refs_1_, bf16[256,2816]{1,0:T(8,128)(2,1)} %get-tuple-element.134.refs_2_, ...), custom_call_target="tpu_custom_call" | custom-call | tf_op jit(solution)/shard_map/outer/pallas_call | solution.py:571
  330.3 7.4 %outer.11 = (bf16[4,4,704,128]{3,2,1,0:T(8,128)(2,1)}, bf16[4,4,704,128]{3,2,1,0:T(8,128)(2,1)}) custom-call(s32[1]{0:T(128)} %bitcast.23.me_ref, bf16[256,1024]{1,0:T(8,128)(2,1)} %multiply_convert_fusion.2.n_ref.refs_0_, bf16[256,1024]{1,0:T(8,128)(2,1)} %get-tuple-element.248.n_ref.refs_1_, bf16[256,2816]{1,0:T(8,128)(2,1)} %get-tuple-element.130.refs_2_, ...), custom_call_target="tpu_custom_call" | custom-call | tf_op jit(solution)/shard_map/outer/pallas_call | solution.py:571
  343.6 17.3 %memory_backward.1 = (bf16[2,4,256,1024]{3,2,1,0:T(8,128)(2,1)}, bf16[4,4,128,128]{3,2,1,0:T(8,128)(2,1)}, bf16[4,4,128,128]{3,2,1,0:T(8,128)(2,1)}, bf16[4,4,12...) custom-call(s32[2]{0:T(128)} %pad_add_fusion.1.place_ref, bf16[2,4,256,1024]{3,2,1,0:T(8,128)(2,1)} %x_ref.5, ...), custom_call_target="tpu_custom_call" | custom-call | tf_op jit(solution)/shard_map/memory_backward/pallas_call | solution.py:682
  382.4 13.3 %collective-permute-done.19 = bf16[2,4,384,128]{3,2,1,0:T(8,128)(2,1)S(1)} collective-permute-done((bf16[2,4,384,128]{3,2,1,0:T(8,128)(2,1)S(1)}, bf16[2,4,384,128]{3,2,1,0:T(8,128)(2,1)S(1)}, u32[]{:S(2)}, u32[]{:S(2)}) %collective-permute-start.19) | collective-permute-done | bytes 786464 | tf_op jit(solution)/shard_map/ppermute | solution.py:708
  399.7 13.8 %collective-permute-done.53 = bf16[2,4,352,128]{3,2,1,0:T(8,128)(2,1)S(1)} collective-permute-done((bf16[2,4,352,128]{3,2,1,0:T(8,128)(2,1)S(1)}, bf16[2,4,352,128]{3,2,1,0:T(8,128)(2,1)S(1)}, u32[]{:S(2)}, u32[]{:S(2)}) %collective-permute-start.53) | collective-permute-done | bytes 720928 | tf_op jit(solution)/shard_map/ppermute | solution.py:708
  416.1 22.0 %collective-permute-done.20 = bf16[1,4,384,128]{3,2,1,0:T(8,128)(2,1)S(1)} collective-permute-done((bf16[1,4,384,128]{3,2,1,0:T(8,128)(2,1)S(1)}, bf16[1,4,384,128]{3,2,1,0:T(8,128)(2,1)S(1)}, u32[]{:S(2)}, u32[]{:S(2)}) %collective-permute-start.20) | collective-permute-done | bytes 393248 | tf_op jit(solution)/shard_map/ppermute | solution.py:708
  447.1 5.1 collective-permute-done.54
  457.9 5.6 collective-permute-done.51
  467.1 28.6 %collective-permute-done.36 = bf16[1,4,128,128]{3,2,1,0:T(8,128)(2,1)S(1)} collective-permute-done((bf16[1,4,128,128]{3,2,1,0:T(8,128)(2,1)S(1)}, bf16[1,4,128,128]{3,2,1,0:T(8,128)(2,1)S(1)}, u32[]{:S(2)}, u32[]{:S(2)}) %collective-permute-start.36) | collective-permute-done | bytes 131104 | tf_op jit(solution)/shard_map/ppermute | solution.py:708
  495.8 14.4 %collective-permute-start.37 = (bf16[1536,128]{1,0:T(8,128)(2,1)S(1)}, bf16[1536,128]{1,0:T(8,128)(2,1)S(1)}, u32[]{:S(2)}, u32[]{:S(2)}) collective-permute-start(bf16[1536,128]{1,0:T(8,128)(2,1)S(1)} %get-tuple-element.214), channel_id=1, source_target_pairs={{0,1},{4,5},{8,9},{12,13},{16,17},{20,21},{24,25},{28,29}} | collective-permute-start | bytes 1179656 | tf_op jit(solution)/shard_map/ppermute | solution.py:760
  547.0 5.7 collective-permute-done.56
  571.2 7.1 %collective-permute-done.60 = bf16[2112,128]{1,0:T(8,128)(2,1)S(1)} collective-permute-done((bf16[2112,128]{1,0:T(8,128)(2,1)S(1)}, bf16[2112,128]{1,0:T(8,128)(2,1)S(1)}, u32[]{:S(2)}, u32[]{:S(2)}) %collective-permute-start.60) | collective-permute-done | bytes 540704 | tf_op jit(solution)/shard_map/ppermute | solution.py:760
  (398 shorter events, 200.0 us)
Async XLA Ops:
  7.2 52.6 %collective-permute-start = (bf16[1,256,1024]{2,1,0:T(8,128)(2,1)}, bf16[1,256,1024]{2,1,0:T(8,128)(2,1)}, u32[]{:S(2)}, u32[]{:S(2)}) collective-permute-start(bf16[1,256,1024]{2,1,0:T(8,128)(2,1)} %get-tuple-element.83), channel_id=1, source_target_pairs={{0,1},{1,2},{2,3},{3,0},{4,5},{5,6},{6,7},{7,4},{8,9},{9,10},{10,1... | collective-permute-start | bytes 1572872 | tf_op jit(solution)/shard_map/ppermute | solution.py:823
  10.3 52.8 %collective-permute-start.1 = (bf16[1,256,1024]{2,1,0:T(8,128)(2,1)}, bf16[1,256,1024]{2,1,0:T(8,128)(2,1)}, u32[]{:S(2)}, u32[]{:S(2)}) collective-permute-start(bf16[1,256,1024]{2,1,0:T(8,128)(2,1)} %get-tuple-element.84), channel_id=1, source_target_pairs={{0,2},{1,3},{2,0},{3,1},{4,6},{5,7},{6,4},{7,5},{8,10},{9,11},{10,... | collective-permute-start | bytes 1572872 | tf_op jit(solution)/shard_map/ppermute | solution.py:823
  12.9 50.2 %collective-permute-start.2 = (bf16[1,256,1024]{2,1,0:T(8,128)(2,1)}, bf16[1,256,1024]{2,1,0:T(8,128)(2,1)}, u32[]{:S(2)}, u32[]{:S(2)}) collective-permute-start(bf16[1,256,1024]{2,1,0:T(8,128)(2,1)} %get-tuple-element.85), channel_id=1, source_target_pairs={{0,3},{1,0},{2,1},{3,2},{4,7},{5,4},{6,5},{7,6},{8,11},{9,8},{10,9... | collective-permute-start | bytes 1572872 | tf_op jit(solution)/shard_map/ppermute | solution.py:823
  20.6 104.9 %collective-permute-start.3 = (bf16[1,256,1024]{2,1,0:T(8,128)(2,1)}, bf16[1,256,1024]{2,1,0:T(8,128)(2,1)}, u32[]{:S(2)}, u32[]{:S(2)}) collective-permute-start(bf16[1,256,1024]{2,1,0:T(8,128)(2,1)} %get-tuple-element.89), channel_id=1, source_target_pairs={{0,1},{1,2},{2,3},{3,0},{4,5},{5,6},{6,7},{7,4},{8,9},{9,10},{10,1... | collective-permute-start | bytes 1572872 | tf_op jit(solution)/shard_map/ppermute | solution.py:823
  21.3 104.2 %collective-permute-start.4 = (bf16[1,256,1024]{2,1,0:T(8,128)(2,1)}, bf16[1,256,1024]{2,1,0:T(8,128)(2,1)}, u32[]{:S(2)}, u32[]{:S(2)}) collective-permute-start(bf16[1,256,1024]{2,1,0:T(8,128)(2,1)} %get-tuple-element.90), channel_id=1, source_target_pairs={{0,2},{1,3},{2,0},{3,1},{4,6},{5,7},{6,4},{7,5},{8,10},{9,11},{10,... | collective-permute-start | bytes 1572872 | tf_op jit(solution)/shard_map/ppermute | solution.py:823
  59.8 65.7 %collective-permute-start.5 = (bf16[1,256,1024]{2,1,0:T(8,128)(2,1)}, bf16[1,256,1024]{2,1,0:T(8,128)(2,1)}, u32[]{:S(2)}, u32[]{:S(2)}) collective-permute-start(bf16[1,256,1024]{2,1,0:T(8,128)(2,1)} %get-tuple-element.91), channel_id=1, source_target_pairs={{0,3},{1,0},{2,1},{3,2},{4,7},{5,4},{6,5},{7,6},{8,11},{9,8},{10,9... | collective-permute-start | bytes 1572872 | tf_op jit(solution)/shard_map/ppermute | solution.py:823
  215.7 20.6 %collective-permute-start.12 = (f32[3584]{0:T(1024)S(1)}, f32[3584]{0:T(1024)S(1)}, u32[]{:S(2)}, u32[]{:S(2)}) collective-permute-start(f32[3584]{0:T(1024)S(1)} %pad_maximum_fusion.8), channel_id=1, source_target_pairs={{0,1},{1,0},{2,3},{3,2},{4,5},{5,4},{6,7},{7,6},{8,9},{9,8},{10,11... | collective-permute-start | bytes 43016 | tf_op jit(solution)/shard_map/ppermute | solution.py:782
  234.2 32.3 %collective-permute-start.6 = (bf16[1,256,1024]{2,1,0:T(8,128)(2,1)}, bf16[1,256,1024]{2,1,0:T(8,128)(2,1)S(1)}, u32[]{:S(2)}, u32[]{:S(2)}) collective-permute-start(bf16[1,256,1024]{2,1,0:T(8,128)(2,1)} %get-tuple-element.105), channel_id=1, source_target_pairs={{0,3},{1,0},{2,1},{3,2},{4,7},{5,4},{6,5},{7,6},{8,11},{9,8},{10,9... | collective-permute-start | bytes 1572872 | tf_op jit(solution)/shard_map/ppermute | solution.py:823
  248.2 38.5 %collective-permute-start.7 = (bf16[1,256,1024]{2,1,0:T(8,128)(2,1)}, bf16[1,256,1024]{2,1,0:T(8,128)(2,1)S(1)}, u32[]{:S(2)}, u32[]{:S(2)}) collective-permute-start(bf16[1,256,1024]{2,1,0:T(8,128)(2,1)} %get-tuple-element.106), channel_id=1, source_target_pairs={{0,2},{1,3},{2,0},{3,1},{4,6},{5,7},{6,4},{7,5},{8,10},{9,11},{10,... | collective-permute-start | bytes 1572872 | tf_op jit(solution)/shard_map/ppermute | solution.py:823
  249.9 36.8 %collective-permute-start.8 = (bf16[1,256,1024]{2,1,0:T(8,128)(2,1)}, bf16[1,256,1024]{2,1,0:T(8,128)(2,1)}, u32[]{:S(2)}, u32[]{:S(2)}) collective-permute-start(bf16[1,256,1024]{2,1,0:T(8,128)(2,1)} %get-tuple-element.107), channel_id=1, source_target_pairs={{0,1},{1,2},{2,3},{3,0},{4,5},{5,6},{6,7},{7,4},{8,9},{9,10},{10,1... | collective-permute-start | bytes 1572872 | tf_op jit(solution)/shard_map/ppermute | solution.py:823
  253.1 55.4 %collective-permute-start.9 = (bf16[1,256,1024]{2,1,0:T(8,128)(2,1)}, bf16[1,256,1024]{2,1,0:T(8,128)(2,1)}, u32[]{:S(2)}, u32[]{:S(2)}) collective-permute-start(bf16[1,256,1024]{2,1,0:T(8,128)(2,1)} %get-tuple-element.109), channel_id=1, source_target_pairs={{0,3},{1,0},{2,1},{3,2},{4,7},{5,4},{6,5},{7,6},{8,11},{9,8},{10,9... | collective-permute-start | bytes 1572872 | tf_op jit(solution)/shard_map/ppermute | solution.py:823
  260.6 48.1 %collective-permute-start.25 = (bf16[4,4,128,128]{3,2,1,0:T(8,128)(2,1)}, bf16[4,4,128,128]{3,2,1,0:T(8,128)(2,1)}, u32[]{:S(2)}, u32[]{:S(2)}) collective-permute-start(bf16[4,4,128,128]{3,2,1,0:T(8,128)(2,1)} %get-tuple-element.123), channel_id=1, source_target_pairs={{0,4},{4,0},{8,12},{12,8},{16,20},{20,16},{24,28},{28,24},{1,5},{5... | collective-permute-start | bytes 1572872 | tf_op jit(solution)/shard_map/ppermute | solution.py:708
  266.5 73.0 %collective-permute-start.18 = (bf16[4,4,128,128]{3,2,1,0:T(8,128)(2,1)}, bf16[4,4,128,128]{3,2,1,0:T(8,128)(2,1)}, u32[]{:S(2)}, u32[]{:S(2)}) collective-permute-start(bf16[4,4,128,128]{3,2,1,0:T(8,128)(2,1)} %get-tuple-element.117), channel_id=1, source_target_pairs={{0,4},{4,0},{8,12},{12,8},{16,20},{20,16},{24,28},{28,24},{1,5},{5... | collective-permute-start | bytes 1572872 | tf_op jit(solution)/shard_map/ppermute | solution.py:708
  286.7 56.4 %collective-permute-start.10 = (bf16[1,256,1024]{2,1,0:T(8,128)(2,1)}, bf16[1,256,1024]{2,1,0:T(8,128)(2,1)}, u32[]{:S(2)}, u32[]{:S(2)}) collective-permute-start(bf16[1,256,1024]{2,1,0:T(8,128)(2,1)} %get-tuple-element.110), channel_id=1, source_target_pairs={{0,2},{1,3},{2,0},{3,1},{4,6},{5,7},{6,4},{7,5},{8,10},{9,11},{10,... | collective-permute-start | bytes 1572872 | tf_op jit(solution)/shard_map/ppermute | solution.py:823
  286.7 56.4 %collective-permute-start.11 = (bf16[1,256,1024]{2,1,0:T(8,128)(2,1)}, bf16[1,256,1024]{2,1,0:T(8,128)(2,1)}, u32[]{:S(2)}, u32[]{:S(2)}) collective-permute-start(bf16[1,256,1024]{2,1,0:T(8,128)(2,1)} %get-tuple-element.111), channel_id=1, source_target_pairs={{0,1},{1,2},{2,3},{3,0},{4,5},{5,6},{6,7},{7,4},{8,9},{9,10},{10,1... | collective-permute-start | bytes 1572872 | tf_op jit(solution)/shard_map/ppermute | solution.py:823
  308.5 54.3 %collective-permute-start.17 = (bf16[4,4,256,128]{3,2,1,0:T(8,128)(2,1)}, bf16[4,4,256,128]{3,2,1,0:T(8,128)(2,1)S(1)}, u32[]{:S(2)}, u32[]{:S(2)}) collective-permute-start(bf16[4,4,256,128]{3,2,1,0:T(8,128)(2,1)} %get-tuple-element.115), channel_id=1, source_target_pairs={{0,4},{4,0},{8,12},{12,8},{16,20},{20,16},{24,28},{28,24},{1,5},{5... | collective-permute-start | bytes 3145736 | tf_op jit(solution)/shard_map/ppermute | solution.py:708
  308.6 52.3 %collective-permute-start.22 = (bf16[4,4,128,128]{3,2,1,0:T(8,128)(2,1)}, bf16[4,4,128,128]{3,2,1,0:T(8,128)(2,1)}, u32[]{:S(2)}, u32[]{:S(2)}) collective-permute-start(bf16[4,4,128,128]{3,2,1,0:T(8,128)(2,1)} %get-tuple-element.121), channel_id=1, source_target_pairs={{0,4},{4,0},{8,12},{12,8},{16,20},{20,16},{24,28},{28,24},{1,5},{5... | collective-permute-start | bytes 1572872 | tf_op jit(solution)/shard_map/ppermute | solution.py:708
  339.5 22.8 %collective-permute-start.26 = (bf16[2,4,128,128]{3,2,1,0:T(8,128)(2,1)}, bf16[2,4,128,128]{3,2,1,0:T(8,128)(2,1)S(1)}, u32[]{:S(2)}, u32[]{:S(2)}) collective-permute-start(bf16[2,4,128,128]{3,2,1,0:T(8,128)(2,1)} %get-tuple-element.225), channel_id=1, source_target_pairs={{0,8},{4,12},{8,0},{12,4},{16,24},{20,28},{24,16},{28,20},{1,9},{5... | collective-permute-start | bytes 786440 | tf_op jit(solution)/shard_map/ppermute | solution.py:708
  343.1 24.2 %collective-permute-start.21 = (bf16[4,4,256,128]{3,2,1,0:T(8,128)(2,1)}, bf16[4,4,256,128]{3,2,1,0:T(8,128)(2,1)}, u32[]{:S(2)}, u32[]{:S(2)}) collective-permute-start(bf16[4,4,256,128]{3,2,1,0:T(8,128)(2,1)} %get-tuple-element.119), channel_id=1, source_target_pairs={{0,4},{4,0},{8,12},{12,8},{16,20},{20,16},{24,28},{28,24},{1,5},{5... | collective-permute-start | bytes 3145736 | tf_op jit(solution)/shard_map/ppermute | solution.py:708
  343.1 36.5 %collective-permute-start.28 = (bf16[4,4,384,128]{3,2,1,0:T(8,128)(2,1)}, bf16[4,4,384,128]{3,2,1,0:T(8,128)(2,1)}, u32[]{:S(2)}, u32[]{:S(2)}) collective-permute-start(bf16[4,4,384,128]{3,2,1,0:T(8,128)(2,1)} %get-tuple-element.125), channel_id=1, source_target_pairs={{0,4},{4,0},{8,12},{12,8},{16,20},{20,16},{24,28},{28,24},{1,5},{5... | collective-permute-start | bytes 4718600 | tf_op jit(solution)/shard_map/ppermute | solution.py:708
  375.1 78.8 %collective-permute-start.46 = (bf16[4,4,704,128]{3,2,1,0:T(8,128)(2,1)S(1)}, bf16[4,4,704,128]{3,2,1,0:T(8,128)(2,1)S(1)}, u32[]{:S(2)}, u32[]{:S(2)}) collective-permute-start(bf16[4,4,704,128]{3,2,1,0:T(8,128)(2,1)S(1)} %copy-done.74), channel_id=1, source_target_pairs={{0,4},{4,0},{8,12},{12,8},{16,20},{20,16},{24,28},{28,24},{1,5},{5... | collective-permute-start | bytes 8650760 | tf_op jit(solution)/shard_map/ppermute | solution.py:708
  375.6 80.5 %collective-permute-start.43 = (bf16[4,4,704,128]{3,2,1,0:T(8,128)(2,1)S(1)}, bf16[4,4,704,128]{3,2,1,0:T(8,128)(2,1)S(1)}, u32[]{:S(2)}, u32[]{:S(2)}) collective-permute-start(bf16[4,4,704,128]{3,2,1,0:T(8,128)(2,1)S(1)} %copy-done.73), channel_id=1, source_target_pairs={{0,4},{4,0},{8,12},{12,8},{16,20},{20,16},{24,28},{28,24},{1,5},{5... | collective-permute-start | bytes 8650760 | tf_op jit(solution)/shard_map/ppermute | solution.py:708
  379.6 33.9 %collective-permute-start.53 = (bf16[2,4,352,128]{3,2,1,0:T(8,128)(2,1)S(1)}, bf16[2,4,352,128]{3,2,1,0:T(8,128)(2,1)S(1)}, u32[]{:S(2)}, u32[]{:S(2)}) collective-permute-start(bf16[2,4,352,128]{3,2,1,0:T(8,128)(2,1)S(1)} %get-tuple-element.203), channel_id=1, source_target_pairs={{0,16},{4,20},{8,24},{12,28},{16,0},{20,4},{24,8},{28,12},{1,17},{... | collective-permute-start | bytes 2162696 | tf_op jit(solution)/shard_map/ppermute | solution.py:708
  398.1 47.3 %collective-permute-start.29 = (bf16[2,4,384,128]{3,2,1,0:T(8,128)(2,1)S(1)}, bf16[2,4,384,128]{3,2,1,0:T(8,128)(2,1)S(1)}, u32[]{:S(2)}, u32[]{:S(2)}) collective-permute-start(bf16[2,4,384,128]{3,2,1,0:T(8,128)(2,1)S(1)} %get-tuple-element.199), channel_id=1, source_target_pairs={{0,16},{4,20},{8,24},{12,28},{16,0},{20,4},{24,8},{28,12},{1,17},{... | collective-permute-start | bytes 2359304 | tf_op jit(solution)/shard_map/ppermute | solution.py:708
  413.6 24.5 %collective-permute-start.20 = (bf16[1,4,384,128]{3,2,1,0:T(8,128)(2,1)S(1)}, bf16[1,4,384,128]{3,2,1,0:T(8,128)(2,1)S(1)}, u32[]{:S(2)}, u32[]{:S(2)}) collective-permute-start(bf16[1,4,384,128]{3,2,1,0:T(8,128)(2,1)S(1)} %add_convert_fusion.27), channel_id=1, source_target_pairs={{0,16},{4,20},{8,24},{12,28},{16,0},{20,4},{24,8},{28,12},{1,17},{... | collective-permute-start | bytes 1179656 | tf_op jit(solution)/shard_map/ppermute | solution.py:708
  415.2 23.6 %collective-permute-start.24 = (bf16[1,4,384,128]{3,2,1,0:T(8,128)(2,1)S(1)}, bf16[1,4,384,128]{3,2,1,0:T(8,128)(2,1)S(1)}, u32[]{:S(2)}, u32[]{:S(2)}) collective-permute-start(bf16[1,4,384,128]{3,2,1,0:T(8,128)(2,1)S(1)} %add_convert_fusion.24), channel_id=1, source_target_pairs={{0,8},{4,12},{8,0},{12,4},{16,24},{20,28},{24,16},{28,20},{1,9},{5... | collective-permute-start | bytes 1179656 | tf_op jit(solution)/shard_map/ppermute | solution.py:708
  438.1 91.6 %collective-permute-start.15 = (f32[3584]{0:T(1024)S(1)}, f32[3584]{0:T(1024)S(1)}, u32[]{:S(2)}, u32[]{:S(2)}) collective-permute-start(f32[3584]{0:T(1024)S(1)} %add.403), channel_id=1, source_target_pairs={{0,8},{4,12},{8,0},{12,4},{16,24},{20,28},{24,16},{28,20},{1,9},{5... | collective-permute-start | bytes 43016 | tf_op jit(solution)/shard_map/ppermute | solution.py:782
  445.4 21.5 %collective-permute-start.33 = (bf16[1,4,128,128]{3,2,1,0:T(8,128)(2,1)S(1)}, bf16[1,4,128,128]{3,2,1,0:T(8,128)(2,1)S(1)}, u32[]{:S(2)}, u32[]{:S(2)}) collective-permute-start(bf16[1,4,128,128]{3,2,1,0:T(8,128)(2,1)S(1)} %add_convert_fusion.49), channel_id=1, source_target_pairs={{0,16},{4,20},{8,24},{12,28},{16,0},{20,4},{24,8},{28,12},{1,17},{... | collective-permute-start | bytes 393224 | tf_op jit(solution)/shard_map/ppermute | solution.py:708
  456.1 54.8 %collective-permute-start.47 = (bf16[2,4,704,128]{3,2,1,0:T(8,128)(2,1)S(1)}, bf16[2,4,704,128]{3,2,1,0:T(8,128)(2,1)S(1)}, u32[]{:S(2)}, u32[]{:S(2)}) collective-permute-start(bf16[2,4,704,128]{3,2,1,0:T(8,128)(2,1)S(1)} %get-tuple-element.197), channel_id=1, source_target_pairs={{0,16},{4,20},{8,24},{12,28},{16,0},{20,4},{24,8},{28,12},{1,17},{... | collective-permute-start | bytes 4325384 | tf_op jit(solution)/shard_map/ppermute | solution.py:708
  463.5 49.0 %collective-permute-start.44 = (bf16[2,4,704,128]{3,2,1,0:T(8,128)(2,1)S(1)}, bf16[2,4,704,128]{3,2,1,0:T(8,128)(2,1)S(1)}, u32[]{:S(2)}, u32[]{:S(2)}) collective-permute-start(bf16[2,4,704,128]{3,2,1,0:T(8,128)(2,1)S(1)} %get-tuple-element.195), channel_id=1, source_target_pairs={{0,8},{4,12},{8,0},{12,4},{16,24},{20,28},{24,16},{28,20},{1,9},{5... | collective-permute-start | bytes 4325384 | tf_op jit(solution)/shard_map/ppermute | solution.py:708
  465.2 30.5 %collective-permute-start.36 = (bf16[1,4,128,128]{3,2,1,0:T(8,128)(2,1)S(1)}, bf16[1,4,128,128]{3,2,1,0:T(8,128)(2,1)S(1)}, u32[]{:S(2)}, u32[]{:S(2)}) collective-permute-start(bf16[1,4,128,128]{3,2,1,0:T(8,128)(2,1)S(1)} %add_convert_fusion.46), channel_id=1, source_target_pairs={{0,8},{4,12},{8,0},{12,4},{16,24},{20,28},{24,16},{28,20},{1,9},{5... | collective-permute-start | bytes 393224 | tf_op jit(solution)/shard_map/ppermute | solution.py:708
  495.8 21.3 %collective-permute-start.37 = (bf16[1536,128]{1,0:T(8,128)(2,1)S(1)}, bf16[1536,128]{1,0:T(8,128)(2,1)S(1)}, u32[]{:S(2)}, u32[]{:S(2)}) collective-permute-start(bf16[1536,128]{1,0:T(8,128)(2,1)S(1)} %get-tuple-element.214), channel_id=1, source_target_pairs={{0,1},{4,5},{8,9},{12,13},{16,17},{20,21},{24,25},{28,29}} | collective-permute-start | bytes 1179656 | tf_op jit(solution)/shard_map/ppermute | solution.py:760
  (106 other events, 932.1 us)
where the time goes:
time: 593 us; the launch traced here: 583 us
  Pallas kernels  195 us (33%)
  waiting for transfers between devices  151 us (25%)
  starting transfers between devices  130 us (22%)
  other arithmetic  45.1 us (8%)
  matrix products  41.8 us (7%)
  local copies, waits for them, and re-layouts  18.3 us (3%)
    ppermute x32, waiting for transfers between devices, swap(): return lax.ppermute(array, 'dp', [(i, i ^ 1 << bit) for i in range(size)])  103 us
    pallas_call x7, Pallas kernels, outer_arranged(): pl.pallas_call(kernel, out_shape=tuple(out_shape), grid_spec=pltpu.Prefet...  44.3 us
    dot_general x18, matrix products, dot32(): lax.dot_general(left, right, (dims, ((), ())), preferred_element_type=jnp...  41.2 us
    ppermute x12, starting transfers between devices, shifted(): lax.ppermute(array, 'mem', [(i, (i + shift) % members) for i in range(mem...  40.8 us
    ppermute x12, starting transfers between devices, along_members(): got[side] = lax.ppermute(sent, 'mem', pairs)  36.7 us
    pallas_call x2, Pallas kernels, feed_forward(): pl.pallas_call(feed_forward_kernel, out_shape=(shape((rows, hidden), jnp....  34.6 us
    pallas_call x2, Pallas kernels, cross_attention_back(): pl.pallas_call(functools.partial(cross_backward_kernel, chunks), out_shap...  34.3 us
    ppermute x32, starting transfers between devices, swap(): return lax.ppermute(array, 'dp', [(i, i ^ 1 << bit) for i in range(size)])  29.9 us
  transfers between devices with their start and end apart: 61, of which 22 were waited for; matrix products, arithmetic and copies ran while one was open for 11% of the time, Pallas kernels for 22%

commit v1 on v0

--- a/solution.py
+++ b/solution.py
@@ -317,7 +317,6 @@
                 pl.BlockSpec((1, 1, 8, length), lambda s, p, _: (s, p, 0, 0)),
             ),
         ),
-        name="self_forward",
     )(counts, q, k, v, base)
 
 
@@ -350,7 +349,6 @@
                 pl.BlockSpec((1, 1, STEP_HEADS, length), lambda s, p, _: (s, p, 0, 0)),
             ),
         ),
-        name="self_backward",
     )(counts, q, k, v, gradient, lse, base)
 
 
@@ -377,7 +375,6 @@
             ),
             scratch_shapes=[pltpu.VMEM((len(pieces), SHARED * length, rows), jnp.float32)],
         ),
-        name="cross_forward",
     )(counts, bases, q, *pieces, *pieces)
 
 
@@ -403,7 +400,6 @@
             ),
             scratch_shapes=[pltpu.VMEM((chunks, rows, SHARED * length), jnp.float32)] * 2,
         ),
-        name="cross_backward",
     )(counts, bases, q, gradient, lse, *pieces, *pieces)
 
 
@@ -425,7 +421,6 @@
         ],
         out_specs=(pl.BlockSpec((rows, tile), lambda f: (0, f)),) * 3
         + (pl.BlockSpec((rows, width), lambda f: (0, 0)),) * 2,
-        name="feed_forward",
     )(rows_normed, branch, w_gate, w_up, w_down)
 
 
@@ -579,7 +574,6 @@
             scratch_shapes=[pltpu.VMEM((features, tokens * len(lefts)), jnp.bfloat16)]
             * (1 + len(orders)),
         ),
-        name="outer",
     )(me, *lefts, *operands)
 
 
@@ -621,7 +615,6 @@
             ],
             out_specs=(pl.BlockSpec(kept, lambda t, _: (0, 0, 0)),) * members,
         ),
-        name="project",
     )(me, memory, c_key, c_value)
     return [found[-1]] + list(found[:-1])
 
@@ -698,7 +691,6 @@
                 pltpu.VMEM((width, both), jnp.float32),
             ],
         ),
-        name="memory_backward",
     )(place, memory, c_key, c_value, *pieces)
     return found[0], found[1:3], found[3:5]
 
@@ -996,9 +988,8 @@
     pairs_b = first_swap([memory_b], 0)
     memory_a = whole_of(later_stages(pairs_a, order_a[1:]))
     memory_b = whole_of(later_stages(pairs_b, order_b[1:]))
-    (rest_a, rest_b), (self_a, self_b), (memory_a, memory_b) = members_sum(
-        [(rest_a, rest_b), (self_a, self_b), (memory_a, memory_b)]
-    )
+    (rest_a, rest_b), (self_a, self_b) = members_sum([(rest_a, rest_b), (self_a, self_b)])
+    ((memory_a, memory_b),) = members_sum([(memory_a, memory_b)])
     tile_rows = share * (width // LANES)
     g_c_out = rows_out(rest_a, share, width, 0)
     g_c_query = rows_out(rest_b, share, width, 0)

time: 593 us -> 597 us (level)
  waiting for transfers between devices: 151 us -> 187 us
  starting transfers between devices: 130 us -> 101 us
    ppermute x12, waiting for transfers between devices: 14.9 us -> 37 us  [shifted(): lax.ppermute(array, 'mem', [(i, (i + shift) % members) for i in range(mem...]
    ppermute x12, starting transfers between devices: 40.8 us -> 19.2 us  [shifted(): lax.ppermute(array, 'mem', [(i, (i + shift) % members) for i in range(mem...]
    ppermute x32, waiting for transfers between devices: 103 us -> 120 us  [swap(): return lax.ppermute(array, 'dp', [(i, i ^ 1 << bit) for i in range(size)])]
    ppermute x32, starting transfers between devices: 29.9 us -> 23.3 us  [swap(): return lax.ppermute(array, 'dp', [(i, i ^ 1 << bit) for i in range(size)])]
    convert_element_type x28 -> x30, other arithmetic: 15.2 us -> 11.1 us  [add16(): (left.astype(jnp.float32) + right.astype(jnp.float32)).astype(jnp.bfloat16)]
    ppermute x12 -> x18, starting transfers between devices: 36.7 us -> 34 us  [along_members(): got[side] = lax.ppermute(sent, 'mem', pairs)]
    ppermute x12 -> x18, waiting for transfers between devices: 23.6 us -> 24.9 us  [along_members(): got[side] = lax.ppermute(sent, 'mem', pairs)]
  transfers between devices with their start and end apart: 61 -> 67, of which waited for: 22 -> 27; matrix products, arithmetic and copies ran while one was open for 11% -> 10% of each run, Pallas kernels for 22% -> 22%
where the time goes in v1:
time: 597 us; the launch traced here: 588 us
  Pallas kernels  195 us (33%)
  waiting for transfers between devices  187 us (31%)
  starting transfers between devices  101 us (17%)
  matrix products  41.8 us (7%)
  other arithmetic  40.6 us (7%)
  local copies, waits for them, and re-layouts  20.9 us (4%)
    ppermute x32, waiting for transfers between devices, swap(): return lax.ppermute(array, 'dp', [(i, i ^ 1 << bit) for i in range(size)])  120 us
    pallas_call x7, Pallas kernels, outer_arranged(): pl.pallas_call(kernel, out_shape=tuple(out_shape), grid_spec=pltpu.Prefet...  44.6 us
    dot_general x18, matrix products, dot32(): lax.dot_general(left, right, (dims, ((), ())), preferred_element_type=jnp...  41.2 us
    ppermute x12, waiting for transfers between devices, shifted(): lax.ppermute(array, 'mem', [(i, (i + shift) % members) for i in range(mem...  37 us
    pallas_call x2, Pallas kernels, feed_forward(): pl.pallas_call(feed_forward_kernel, out_shape=(shape((rows, hidden), jnp....  34.6 us
    pallas_call x2, Pallas kernels, cross_attention_back(): pl.pallas_call(functools.partial(cross_backward_kernel, chunks), out_shap...  34.3 us
    ppermute x18, starting transfers between devices, along_members(): got[side] = lax.ppermute(sent, 'mem', pairs)  34 us
    ppermute x18, waiting for transfers between devices, along_members(): got[side] = lax.ppermute(sent, 'mem', pairs)  24.9 us
  transfers between devices with their start and end apart: 67, of which 27 were waited for; matrix products, arithmetic and copies ran while one was open for 10% of the time, Pallas kernels for 22%

profile of v1, /device:TPU:0, one launch (start us, length us, event | category | flops | bytes accessed | tf_op | source)
XLA Modules:
  0.0 588.1 jit_solution(7597528858904043977)
XLA Ops:
  0.7 6.5 %shard_map.359 = (bf16[1,256,1024]{2,1,0:T(8,128)(2,1)}, bf16[1,256,1024]{2,1,0:T(8,128)(2,1)}, bf16[1,256,1024]{2,1,0:T(8,128)(2,1)}, bf16[1,256,1024]{2,1,0:T(8,128)(2,1)}) custom-call(s32[1]{0:T(128)} %bitcast.10.place_ref, bf16[2,4,256,1024]{3,2,1,0:T(8,128)(2,1)} %x_ref.5, bf16[1024,512]{1,0:T(8,128)(2,1)} %ck_ref.5, bf16[1024,512]{1,0:T(8,128)(2,1)} %cv_ref.5), custom_call_target="tpu_custom_call" | custom-call | tf_op jit(solution)/shard_map/pallas_call | solution.py:602
  14.2 6.3 %shard_map.362 = (bf16[1,256,1024]{2,1,0:T(8,128)(2,1)}, bf16[1,256,1024]{2,1,0:T(8,128)(2,1)}, bf16[1,256,1024]{2,1,0:T(8,128)(2,1)}, bf16[1,256,1024]{2,1,0:T(8,128)(2,1)}) custom-call(s32[1]{0:T(128)} %bitcast.10.place_ref, bf16[2,4,256,1024]{3,2,1,0:T(8,128)(2,1)} %x_ref.5, bf16[1024,512]{1,0:T(8,128)(2,1)} %ck_ref.5, bf16[1024,512]{1,0:T(8,128)(2,1)} %cv_ref.5), custom_call_target="tpu_custom_call" | custom-call | tf_op jit(solution)/shard_map/pallas_call | solution.py:602
  31.0 14.6 %shard_map.358 = (bf16[512,1024]{1,0:T(8,128)(2,1)}, f32[2,4,8,256]{3,2,1,0:T(8,128)}) custom-call(s32[2]{0:T(128)} %bitcast.309, bf16[512,1024]{1,0:T(8,128)(2,1)} %convolution_convert_fusion.q_ref, bf16[512,512]{1,0:T(8,128)(2,1)} %convolution_convert_fusion.8.k_ref, bf16[512,512]{1,0:T(8,128)(2,1)} %convolution_convert_fusion.7.v_ref, ...), custom_call_target="tpu_custom_call" | custom-call | tf_op jit(solution)/shard_map/pallas_call | solution.py:303
  63.0 12.2 %shard_map.360 = (bf16[256,1024]{1,0:T(8,128)(2,1)}, f32[1,4,8,256]{3,2,1,0:T(8,128)}) custom-call(s32[1]{0:T(128)} %bitcast.5.count_ref, s32[4]{0:T(128)} %pad_add_fusion.base_ref, bf16[256,1024]{1,0:T(8,128)(2,1)} %convolution_convert_fusion.6.q_ref, bf16[1,256,1024]{2,1,0:T(8,128)(2,1)} %get-tuple-element.82.refs_0_.refs_4_, ...), custom_call_target="tpu_custom_call" | custom-call | tf_op jit(solution)/shard_map/pallas_call | solution.py:365
  79.9 17.3 %shard_map.361 = (bf16[256,2816]{1,0:T(8,128)(2,1)}, bf16[256,2816]{1,0:T(8,128)(2,1)}, bf16[256,2816]{1,0:T(8,128)(2,1)}, f32[256,1024]{1,0:T(8,128)}, f32[256,1024]{1,0:T(8,128)}) custom-call(bf16[256,1024]{1,0:T(8,128)(2,1)} %multiply_convert_fusion.2.n_ref.refs_0_, bf16[256,1024]{1,0:T(8,128)(2,1)} %get-tuple-element.234.b_ref.refs_2_.refs_4_, ...), custom_call_target="tpu_custom_call" | custom-call | tf_op jit(solution)/shard_map/pallas_call | solution.py:410
  102.6 17.0 %shard_map.365 = (bf16[256,1024]{1,0:T(8,128)(2,1)}, bf16[1,256,1024]{2,1,0:T(8,128)(2,1)}, bf16[1,256,1024]{2,1,0:T(8,128)(2,1)}, bf16[1,256,1024]{2,1,0:T(8,128)(2,1)}, bf16[1,256,1024]{2,1,0:T(8,128)(2,1)}) custom-call(s32[1]{0:T(128)} %bitcast.5.count_ref, s32[4]{0:T(128)} %pad_add_fusion.base_ref, bf16[256,1024]{1,0:T(8,128)(2,1)} %convolution_convert_fusion.6.q_ref, ...), custom_call_target="tpu_custom_call" | custom-call | tf_op jit(solution)/shard_map/pallas_call | solution.py:384
  125.3 12.3 %shard_map.363 = (bf16[256,1024]{1,0:T(8,128)(2,1)}, f32[1,4,8,256]{3,2,1,0:T(8,128)}) custom-call(s32[1]{0:T(128)} %bitcast.15.count_ref, s32[4]{0:T(128)} %pad_add_fusion.base_ref, bf16[256,1024]{1,0:T(8,128)(2,1)} %convolution_convert_fusion.5.q_ref, bf16[1,256,1024]{2,1,0:T(8,128)(2,1)} %get-tuple-element.88.refs_0_.refs_4_, ...), custom_call_target="tpu_custom_call" | custom-call | tf_op jit(solution)/shard_map/pallas_call | solution.py:365
  144.2 17.3 %shard_map.364 = (bf16[256,2816]{1,0:T(8,128)(2,1)}, bf16[256,2816]{1,0:T(8,128)(2,1)}, bf16[256,2816]{1,0:T(8,128)(2,1)}, f32[256,1024]{1,0:T(8,128)}, f32[256,1024]{1,0:T(8,128)}) custom-call(bf16[256,1024]{1,0:T(8,128)(2,1)} %get-tuple-element.254.n_ref.refs_1_, bf16[256,1024]{1,0:T(8,128)(2,1)} %get-tuple-element.235.b_ref.refs_3_.refs_5_, ...), custom_call_target="tpu_custom_call" | custom-call | tf_op jit(solution)/shard_map/pallas_call | solution.py:410
  166.9 17.2 %shard_map.366 = (bf16[256,1024]{1,0:T(8,128)(2,1)}, bf16[1,256,1024]{2,1,0:T(8,128)(2,1)}, bf16[1,256,1024]{2,1,0:T(8,128)(2,1)}, bf16[1,256,1024]{2,1,0:T(8,128)(2,1)}, bf16[1,256,1024]{2,1,0:T(8,128)(2,1)}) custom-call(s32[1]{0:T(128)} %bitcast.15.count_ref, s32[4]{0:T(128)} %pad_add_fusion.base_ref, bf16[256,1024]{1,0:T(8,128)(2,1)} %convolution_convert_fusion.5.q_ref, ...), custom_call_target="tpu_custom_call" | custom-call | tf_op jit(solution)/shard_map/pallas_call | solution.py:384
  191.1 12.1 %shard_map.367 = (bf16[512,1024]{1,0:T(8,128)(2,1)}, bf16[512,512]{1,0:T(8,128)(2,1)}, bf16[512,512]{1,0:T(8,128)(2,1)}, f32[2,4,4,256]{3,2,1,0:T(4,128)}) custom-call(s32[2]{0:T(128)} %bitcast.310, bf16[512,1024]{1,0:T(8,128)(2,1)} %convolution_convert_fusion.q_ref, bf16[512,512]{1,0:T(8,128)(2,1)} %convolution_convert_fusion.8.k_ref, ...), custom_call_target="tpu_custom_call" | custom-call | tf_op jit(solution)/shard_map/pallas_call | solution.py:326
  210.5 5.0 fusion.7
  215.5 18.4 %collective-permute-start.12 = (f32[3584]{0:T(1024)S(1)}, f32[3584]{0:T(1024)S(1)}, u32[]{:S(2)}, u32[]{:S(2)}) collective-permute-start(f32[3584]{0:T(1024)S(1)} %pad_maximum_fusion.9), channel_id=1, source_target_pairs={{0,1},{1,0},{2,3},{3,2},{4,5},{5,4},{6,7},{7,6},{8,9},{9,8},{10,11... | collective-permute-start | bytes 43016 | tf_op jit(solution)/shard_map/ppermute | solution.py:774
  243.5 6.8 %shard_map.372 = (bf16[4,4,128,128]{3,2,1,0:T(8,128)(2,1)}, bf16[4,4,128,128]{3,2,1,0:T(8,128)(2,1)}, bf16[4,4,384,128]{3,2,1,0:T(8,128)(2,1)}, bf16[4,4,384,128]{3,2,1,0:T(8,128)(2,1)}) custom-call(s32[1]{0:T(128)} %bitcast.23.me_ref, bf16[512,1024]{1,0:T(8,128)(2,1)} %copy-done.25, bf16[512,512]{1,0:T(8,128)(2,1)} %get-tuple-element.102.refs_1_, ...), custom_call_target="tpu_custom_call" | custom-call | tf_op jit(solution)/shard_map/pallas_call | solution.py:566
  263.2 4.9 shard_map.370
  269.4 31.3 %collective-permute-done.7.refs_2_ = bf16[1,256,1024]{2,1,0:T(8,128)(2,1)} collective-permute-done((bf16[1,256,1024]{2,1,0:T(8,128)(2,1)}, bf16[1,256,1024]{2,1,0:T(8,128)(2,1)}, u32[]{:S(2)}, u32[]{:S(2)}) %collective-permute-start.7) | collective-permute-done | bytes 524320 | tf_op jit(solution)/shard_map/ppermute | solution.py:815
  310.8 9.2 %shard_map.375 = (bf16[4,4,352,128]{3,2,1,0:T(8,128)(2,1)}, bf16[4,4,352,128]{3,2,1,0:T(8,128)(2,1)}, bf16[4,4,352,128]{3,2,1,0:T(8,128)(2,1)}, bf16[4,4,352,128]{3,2,1,0:T(8,128)(2,1)}) custom-call(s32[1]{0:T(128)} %bitcast.23.me_ref, bf16[256,2816]{1,0:T(8,128)(2,1)} %get-tuple-element.138.refs_0_, bf16[256,2816]{1,0:T(8,128)(2,1)} %get-tuple-element.139.refs_1_, ...), custom_call_target="tpu_custom_call" | custom-call | tf_op jit(solution)/shard_map/pallas_call | solution.py:566
  320.0 7.4 %shard_map.374 = (bf16[4,4,704,128]{3,2,1,0:T(8,128)(2,1)}, bf16[4,4,704,128]{3,2,1,0:T(8,128)(2,1)}) custom-call(s32[1]{0:T(128)} %bitcast.23.me_ref, bf16[256,1024]{1,0:T(8,128)(2,1)} %multiply_convert_fusion.2.n_ref.refs_0_, bf16[256,1024]{1,0:T(8,128)(2,1)} %get-tuple-element.254.n_ref.refs_1_, bf16[256,2816]{1,0:T(8,128)(2,1)} %get-tuple-element.134.refs_2_, ...), custom_call_target="tpu_custom_call" | custom-call | tf_op jit(solution)/shard_map/pallas_call | solution.py:566
  327.4 7.3 %shard_map.373 = (bf16[4,4,704,128]{3,2,1,0:T(8,128)(2,1)}, bf16[4,4,704,128]{3,2,1,0:T(8,128)(2,1)}) custom-call(s32[1]{0:T(128)} %bitcast.23.me_ref, bf16[256,1024]{1,0:T(8,128)(2,1)} %multiply_convert_fusion.2.n_ref.refs_0_, bf16[256,1024]{1,0:T(8,128)(2,1)} %get-tuple-element.254.n_ref.refs_1_, bf16[256,2816]{1,0:T(8,128)(2,1)} %get-tuple-element.130.refs_2_, ...), custom_call_target="tpu_custom_call" | custom-call | tf_op jit(solution)/shard_map/pallas_call | solution.py:566
  339.1 5.6 collective-permute-done.10.refs_6_
  346.3 17.3 %shard_map.368 = (bf16[2,4,256,1024]{3,2,1,0:T(8,128)(2,1)}, bf16[4,4,128,128]{3,2,1,0:T(8,128)(2,1)}, bf16[4,4,128,128]{3,2,1,0:T(8,128)(2,1)}, bf16[4,4,128,12...) custom-call(s32[2]{0:T(128)} %pad_add_fusion.1.place_ref, bf16[2,4,256,1024]{3,2,1,0:T(8,128)(2,1)} %x_ref.5, ...), custom_call_target="tpu_custom_call" | custom-call | tf_op jit(solution)/shard_map/pallas_call | solution.py:675
  403.0 16.3 %collective-permute-done.23 = bf16[2,4,384,128]{3,2,1,0:T(8,128)(2,1)S(1)} collective-permute-done((bf16[2,4,384,128]{3,2,1,0:T(8,128)(2,1)S(1)}, bf16[2,4,384,128]{3,2,1,0:T(8,128)(2,1)S(1)}, u32[]{:S(2)}, u32[]{:S(2)}) %collective-permute-start.23) | collective-permute-done | bytes 786464 | tf_op jit(solution)/shard_map/ppermute | solution.py:700
  421.9 12.9 %collective-permute-done.59 = bf16[2,4,352,128]{3,2,1,0:T(8,128)(2,1)S(1)} collective-permute-done((bf16[2,4,352,128]{3,2,1,0:T(8,128)(2,1)S(1)}, bf16[2,4,352,128]{3,2,1,0:T(8,128)(2,1)S(1)}, u32[]{:S(2)}, u32[]{:S(2)}) %collective-permute-start.59) | collective-permute-done | bytes 720928 | tf_op jit(solution)/shard_map/ppermute | solution.py:700
  438.2 6.8 %collective-permute-done.24 = bf16[1,4,384,128]{3,2,1,0:T(8,128)(2,1)S(1)} collective-permute-done((bf16[1,4,384,128]{3,2,1,0:T(8,128)(2,1)S(1)}, bf16[1,4,384,128]{3,2,1,0:T(8,128)(2,1)S(1)}, u32[]{:S(2)}, u32[]{:S(2)}) %collective-permute-start.24) | collective-permute-done | bytes 393248 | tf_op jit(solution)/shard_map/ppermute | solution.py:700
  446.7 12.8 %collective-permute-done.20 = bf16[1,4,384,128]{3,2,1,0:T(8,128)(2,1)S(1)} collective-permute-done((bf16[1,4,384,128]{3,2,1,0:T(8,128)(2,1)S(1)}, bf16[1,4,384,128]{3,2,1,0:T(8,128)(2,1)S(1)}, u32[]{:S(2)}, u32[]{:S(2)}) %collective-permute-start.20) | collective-permute-done | bytes 393248 | tf_op jit(solution)/shard_map/ppermute | solution.py:700
  466.1 4.7 collective-permute-done.60
  472.7 6.6 %collective-permute-done.30 = bf16[1,4,384,128]{3,2,1,0:T(8,128)(2,1)S(1)} collective-permute-done((bf16[1,4,384,128]{3,2,1,0:T(8,128)(2,1)S(1)}, bf16[1,4,384,128]{3,2,1,0:T(8,128)(2,1)S(1)}, u32[]{:S(2)}, u32[]{:S(2)}) %collective-permute-start.30) | collective-permute-done | bytes 393248 | tf_op jit(solution)/shard_map/ppermute | solution.py:700
  480.9 20.3 %collective-permute-done.53 = bf16[2,4,704,128]{3,2,1,0:T(8,128)(2,1)S(1)} collective-permute-done((bf16[2,4,704,128]{3,2,1,0:T(8,128)(2,1)S(1)}, bf16[2,4,704,128]{3,2,1,0:T(8,128)(2,1)S(1)}, u32[]{:S(2)}, u32[]{:S(2)}) %collective-permute-start.53) | collective-permute-done | bytes 1441824 | tf_op jit(solution)/shard_map/ppermute | solution.py:700
  502.1 6.8 %collective-permute-done.50 = bf16[2,4,704,128]{3,2,1,0:T(8,128)(2,1)S(1)} collective-permute-done((bf16[2,4,704,128]{3,2,1,0:T(8,128)(2,1)S(1)}, bf16[2,4,704,128]{3,2,1,0:T(8,128)(2,1)S(1)}, u32[]{:S(2)}, u32[]{:S(2)}) %collective-permute-start.50) | collective-permute-done | bytes 1441824 | tf_op jit(solution)/shard_map/ppermute | solution.py:700
  511.5 14.2 %collective-permute-done.54 = bf16[1,4,704,128]{3,2,1,0:T(8,128)(2,1)S(1)} collective-permute-done((bf16[1,4,704,128]{3,2,1,0:T(8,128)(2,1)S(1)}, bf16[1,4,704,128]{3,2,1,0:T(8,128)(2,1)S(1)}, u32[]{:S(2)}, u32[]{:S(2)}) %collective-permute-start.54) | collective-permute-done | bytes 720928 | tf_op jit(solution)/shard_map/ppermute | solution.py:700
  539.7 4.9 collective-permute-done.61
  552.6 8.7 %collective-permute-done.62 = bf16[2112,128]{1,0:T(8,128)(2,1)S(1)} collective-permute-done((bf16[2112,128]{1,0:T(8,128)(2,1)S(1)}, bf16[2112,128]{1,0:T(8,128)(2,1)S(1)}, u32[]{:S(2)}, u32[]{:S(2)}) %collective-permute-start.62) | collective-permute-done | bytes 540704 | tf_op jit(solution)/shard_map/ppermute | solution.py:752
  577.1 7.7 %collective-permute-done.66 = bf16[2112,128]{1,0:T(8,128)(2,1)S(1)} collective-permute-done((bf16[2112,128]{1,0:T(8,128)(2,1)S(1)}, bf16[2112,128]{1,0:T(8,128)(2,1)S(1)}, u32[]{:S(2)}, u32[]{:S(2)}) %collective-permute-start.66) | collective-permute-done | bytes 540704 | tf_op jit(solution)/shard_map/ppermute | solution.py:752
  (406 shorter events, 216.9 us)
Async XLA Ops:
  7.2 52.6 %collective-permute-start = (bf16[1,256,1024]{2,1,0:T(8,128)(2,1)}, bf16[1,256,1024]{2,1,0:T(8,128)(2,1)}, u32[]{:S(2)}, u32[]{:S(2)}) collective-permute-start(bf16[1,256,1024]{2,1,0:T(8,128)(2,1)} %get-tuple-element.83), channel_id=1, source_target_pairs={{0,1},{1,2},{2,3},{3,0},{4,5},{5,6},{6,7},{7,4},{8,9},{9,10},{10,1... | collective-permute-start | bytes 1572872 | tf_op jit(solution)/shard_map/ppermute | solution.py:815
  10.2 52.8 %collective-permute-start.1 = (bf16[1,256,1024]{2,1,0:T(8,128)(2,1)}, bf16[1,256,1024]{2,1,0:T(8,128)(2,1)}, u32[]{:S(2)}, u32[]{:S(2)}) collective-permute-start(bf16[1,256,1024]{2,1,0:T(8,128)(2,1)} %get-tuple-element.84), channel_id=1, source_target_pairs={{0,2},{1,3},{2,0},{3,1},{4,6},{5,7},{6,4},{7,5},{8,10},{9,11},{10,... | collective-permute-start | bytes 1572872 | tf_op jit(solution)/shard_map/ppermute | solution.py:815
  12.8 50.2 %collective-permute-start.2 = (bf16[1,256,1024]{2,1,0:T(8,128)(2,1)}, bf16[1,256,1024]{2,1,0:T(8,128)(2,1)}, u32[]{:S(2)}, u32[]{:S(2)}) collective-permute-start(bf16[1,256,1024]{2,1,0:T(8,128)(2,1)} %get-tuple-element.85), channel_id=1, source_target_pairs={{0,3},{1,0},{2,1},{3,2},{4,7},{5,4},{6,5},{7,6},{8,11},{9,8},{10,9... | collective-permute-start | bytes 1572872 | tf_op jit(solution)/shard_map/ppermute | solution.py:815
  20.5 104.8 %collective-permute-start.3 = (bf16[1,256,1024]{2,1,0:T(8,128)(2,1)}, bf16[1,256,1024]{2,1,0:T(8,128)(2,1)}, u32[]{:S(2)}, u32[]{:S(2)}) collective-permute-start(bf16[1,256,1024]{2,1,0:T(8,128)(2,1)} %get-tuple-element.89), channel_id=1, source_target_pairs={{0,1},{1,2},{2,3},{3,0},{4,5},{5,6},{6,7},{7,4},{8,9},{9,10},{10,1... | collective-permute-start | bytes 1572872 | tf_op jit(solution)/shard_map/ppermute | solution.py:815
  21.1 104.1 %collective-permute-start.4 = (bf16[1,256,1024]{2,1,0:T(8,128)(2,1)}, bf16[1,256,1024]{2,1,0:T(8,128)(2,1)}, u32[]{:S(2)}, u32[]{:S(2)}) collective-permute-start(bf16[1,256,1024]{2,1,0:T(8,128)(2,1)} %get-tuple-element.90), channel_id=1, source_target_pairs={{0,2},{1,3},{2,0},{3,1},{4,6},{5,7},{6,4},{7,5},{8,10},{9,11},{10,... | collective-permute-start | bytes 1572872 | tf_op jit(solution)/shard_map/ppermute | solution.py:815
  59.7 65.5 %collective-permute-start.5 = (bf16[1,256,1024]{2,1,0:T(8,128)(2,1)}, bf16[1,256,1024]{2,1,0:T(8,128)(2,1)}, u32[]{:S(2)}, u32[]{:S(2)}) collective-permute-start(bf16[1,256,1024]{2,1,0:T(8,128)(2,1)} %get-tuple-element.91), channel_id=1, source_target_pairs={{0,3},{1,0},{2,1},{3,2},{4,7},{5,4},{6,5},{7,6},{8,11},{9,8},{10,9... | collective-permute-start | bytes 1572872 | tf_op jit(solution)/shard_map/ppermute | solution.py:815
  254.7 46.1 %collective-permute-start.7 = (bf16[1,256,1024]{2,1,0:T(8,128)(2,1)}, bf16[1,256,1024]{2,1,0:T(8,128)(2,1)}, u32[]{:S(2)}, u32[]{:S(2)}) collective-permute-start(bf16[1,256,1024]{2,1,0:T(8,128)(2,1)} %get-tuple-element.106), channel_id=1, source_target_pairs={{0,2},{1,3},{2,0},{3,1},{4,6},{5,7},{6,4},{7,5},{8,10},{9,11},{10,... | collective-permute-start | bytes 1572872 | tf_op jit(solution)/shard_map/ppermute | solution.py:815
  254.7 46.1 %collective-permute-start.25 = (bf16[4,4,128,128]{3,2,1,0:T(8,128)(2,1)}, bf16[4,4,128,128]{3,2,1,0:T(8,128)(2,1)}, u32[]{:S(2)}, u32[]{:S(2)}) collective-permute-start(bf16[4,4,128,128]{3,2,1,0:T(8,128)(2,1)} %get-tuple-element.123), channel_id=1, source_target_pairs={{0,4},{4,0},{8,12},{12,8},{16,20},{20,16},{24,28},{28,24},{1,5},{5... | collective-permute-start | bytes 1572872 | tf_op jit(solution)/shard_map/ppermute | solution.py:700
  256.3 80.4 %collective-permute-start.8 = (bf16[1,256,1024]{2,1,0:T(8,128)(2,1)}, bf16[1,256,1024]{2,1,0:T(8,128)(2,1)}, u32[]{:S(2)}, u32[]{:S(2)}) collective-permute-start(bf16[1,256,1024]{2,1,0:T(8,128)(2,1)} %get-tuple-element.107), channel_id=1, source_target_pairs={{0,1},{1,2},{2,3},{3,0},{4,5},{5,6},{6,7},{7,4},{8,9},{9,10},{10,1... | collective-permute-start | bytes 1572872 | tf_op jit(solution)/shard_map/ppermute | solution.py:815
  258.5 78.7 %collective-permute-start.9 = (bf16[1,256,1024]{2,1,0:T(8,128)(2,1)}, bf16[1,256,1024]{2,1,0:T(8,128)(2,1)}, u32[]{:S(2)}, u32[]{:S(2)}) collective-permute-start(bf16[1,256,1024]{2,1,0:T(8,128)(2,1)} %get-tuple-element.109), channel_id=1, source_target_pairs={{0,3},{1,0},{2,1},{3,2},{4,7},{5,4},{6,5},{7,6},{8,11},{9,8},{10,9... | collective-permute-start | bytes 1572872 | tf_op jit(solution)/shard_map/ppermute | solution.py:815
  268.1 76.6 %collective-permute-start.10 = (bf16[1,256,1024]{2,1,0:T(8,128)(2,1)}, bf16[1,256,1024]{2,1,0:T(8,128)(2,1)S(1)}, u32[]{:S(2)}, u32[]{:S(2)}) collective-permute-start(bf16[1,256,1024]{2,1,0:T(8,128)(2,1)} %get-tuple-element.110), channel_id=1, source_target_pairs={{0,2},{1,3},{2,0},{3,1},{4,6},{5,7},{6,4},{7,5},{8,10},{9,11},{10,... | collective-permute-start | bytes 1572872 | tf_op jit(solution)/shard_map/ppermute | solution.py:815
  300.8 43.9 %collective-permute-start.11 = (bf16[1,256,1024]{2,1,0:T(8,128)(2,1)}, bf16[1,256,1024]{2,1,0:T(8,128)(2,1)S(1)}, u32[]{:S(2)}, u32[]{:S(2)}) collective-permute-start(bf16[1,256,1024]{2,1,0:T(8,128)(2,1)} %get-tuple-element.111), channel_id=1, source_target_pairs={{0,1},{1,2},{2,3},{3,0},{4,5},{5,6},{6,7},{7,4},{8,9},{9,10},{10,1... | collective-permute-start | bytes 1572872 | tf_op jit(solution)/shard_map/ppermute | solution.py:815
  300.8 62.9 %collective-permute-start.22 = (bf16[4,4,128,128]{3,2,1,0:T(8,128)(2,1)}, bf16[4,4,128,128]{3,2,1,0:T(8,128)(2,1)}, u32[]{:S(2)}, u32[]{:S(2)}) collective-permute-start(bf16[4,4,128,128]{3,2,1,0:T(8,128)(2,1)} %get-tuple-element.121), channel_id=1, source_target_pairs={{0,4},{4,0},{8,12},{12,8},{16,20},{20,16},{24,28},{28,24},{1,5},{5... | collective-permute-start | bytes 1572872 | tf_op jit(solution)/shard_map/ppermute | solution.py:700
  336.7 29.1 %collective-permute-start.18 = (bf16[4,4,128,128]{3,2,1,0:T(8,128)(2,1)}, bf16[4,4,128,128]{3,2,1,0:T(8,128)(2,1)}, u32[]{:S(2)}, u32[]{:S(2)}) collective-permute-start(bf16[4,4,128,128]{3,2,1,0:T(8,128)(2,1)} %get-tuple-element.117), channel_id=1, source_target_pairs={{0,4},{4,0},{8,12},{12,8},{16,20},{20,16},{24,28},{28,24},{1,5},{5... | collective-permute-start | bytes 1572872 | tf_op jit(solution)/shard_map/ppermute | solution.py:700
  337.2 28.5 %collective-permute-start.26 = (bf16[2,4,128,128]{3,2,1,0:T(8,128)(2,1)}, bf16[2,4,128,128]{3,2,1,0:T(8,128)(2,1)S(1)}, u32[]{:S(2)}, u32[]{:S(2)}) collective-permute-start(bf16[2,4,128,128]{3,2,1,0:T(8,128)(2,1)} %get-tuple-element.231), channel_id=1, source_target_pairs={{0,8},{4,12},{8,0},{12,4},{16,24},{20,28},{24,16},{28,20},{1,9},{5... | collective-permute-start | bytes 786440 | tf_op jit(solution)/shard_map/ppermute | solution.py:700
  344.7 28.1 %collective-permute-start.21 = (bf16[4,4,256,128]{3,2,1,0:T(8,128)(2,1)}, bf16[4,4,256,128]{3,2,1,0:T(8,128)(2,1)S(1)}, u32[]{:S(2)}, u32[]{:S(2)}) collective-permute-start(bf16[4,4,256,128]{3,2,1,0:T(8,128)(2,1)} %get-tuple-element.119), channel_id=1, source_target_pairs={{0,4},{4,0},{8,12},{12,8},{16,20},{20,16},{24,28},{28,24},{1,5},{5... | collective-permute-start | bytes 3145736 | tf_op jit(solution)/shard_map/ppermute | solution.py:700
  346.3 29.0 %collective-permute-start.17 = (bf16[4,4,256,128]{3,2,1,0:T(8,128)(2,1)}, bf16[4,4,256,128]{3,2,1,0:T(8,128)(2,1)S(1)}, u32[]{:S(2)}, u32[]{:S(2)}) collective-permute-start(bf16[4,4,256,128]{3,2,1,0:T(8,128)(2,1)} %get-tuple-element.115), channel_id=1, source_target_pairs={{0,4},{4,0},{8,12},{12,8},{16,20},{20,16},{24,28},{28,24},{1,5},{5... | collective-permute-start | bytes 3145736 | tf_op jit(solution)/shard_map/ppermute | solution.py:700
  371.7 29.9 %collective-permute-start.28 = (bf16[4,4,384,128]{3,2,1,0:T(8,128)(2,1)S(1)}, bf16[4,4,384,128]{3,2,1,0:T(8,128)(2,1)S(1)}, u32[]{:S(2)}, u32[]{:S(2)}) collective-permute-start(bf16[4,4,384,128]{3,2,1,0:T(8,128)(2,1)S(1)} %copy-done.70), channel_id=1, source_target_pairs={{0,4},{4,0},{8,12},{12,8},{16,20},{20,16},{24,28},{28,24},{1,5},{5... | collective-permute-start | bytes 4718600 | tf_op jit(solution)/shard_map/ppermute | solution.py:700
  371.8 24.6 %collective-permute-start.58 = (bf16[4,4,352,128]{3,2,1,0:T(8,128)(2,1)}, bf16[4,4,352,128]{3,2,1,0:T(8,128)(2,1)S(1)}, u32[]{:S(2)}, u32[]{:S(2)}) collective-permute-start(bf16[4,4,352,128]{3,2,1,0:T(8,128)(2,1)} %get-tuple-element.143), channel_id=1, source_target_pairs={{0,4},{4,0},{8,12},{12,8},{16,20},{20,16},{24,28},{28,24},{1,5},{5... | collective-permute-start | bytes 4325384 | tf_op jit(solution)/shard_map/ppermute | solution.py:700
  372.5 25.0 %collective-permute-start.55 = (bf16[4,4,352,128]{3,2,1,0:T(8,128)(2,1)S(1)}, bf16[4,4,352,128]{3,2,1,0:T(8,128)(2,1)S(1)}, u32[]{:S(2)}, u32[]{:S(2)}) collective-permute-start(bf16[4,4,352,128]{3,2,1,0:T(8,128)(2,1)S(1)} %copy-done.71), channel_id=1, source_target_pairs={{0,4},{4,0},{8,12},{12,8},{16,20},{20,16},{24,28},{28,24},{1,5},{5... | collective-permute-start | bytes 4325384 | tf_op jit(solution)/shard_map/ppermute | solution.py:700
  381.6 80.7 %collective-permute-start.52 = (bf16[4,4,704,128]{3,2,1,0:T(8,128)(2,1)S(1)}, bf16[4,4,704,128]{3,2,1,0:T(8,128)(2,1)S(1)}, u32[]{:S(2)}, u32[]{:S(2)}) collective-permute-start(bf16[4,4,704,128]{3,2,1,0:T(8,128)(2,1)S(1)} %copy-done.68), channel_id=1, source_target_pairs={{0,4},{4,0},{8,12},{12,8},{16,20},{20,16},{24,28},{28,24},{1,5},{5... | collective-permute-start | bytes 8650760 | tf_op jit(solution)/shard_map/ppermute | solution.py:700
  398.9 65.4 %collective-permute-start.49 = (bf16[4,4,704,128]{3,2,1,0:T(8,128)(2,1)S(1)}, bf16[4,4,704,128]{3,2,1,0:T(8,128)(2,1)S(1)}, u32[]{:S(2)}, u32[]{:S(2)}) collective-permute-start(bf16[4,4,704,128]{3,2,1,0:T(8,128)(2,1)S(1)} %copy-done.67), channel_id=1, source_target_pairs={{0,4},{4,0},{8,12},{12,8},{16,20},{20,16},{24,28},{28,24},{1,5},{5... | collective-permute-start | bytes 8650760 | tf_op jit(solution)/shard_map/ppermute | solution.py:700
  398.9 20.4 %collective-permute-start.23 = (bf16[2,4,384,128]{3,2,1,0:T(8,128)(2,1)S(1)}, bf16[2,4,384,128]{3,2,1,0:T(8,128)(2,1)S(1)}, u32[]{:S(2)}, u32[]{:S(2)}) collective-permute-start(bf16[2,4,384,128]{3,2,1,0:T(8,128)(2,1)S(1)} %pad_maximum_fusion.4), channel_id=1, source_target_pairs={{0,16},{4,20},{8,24},{12,28},{16,0},{20,4},{24,8},{28,12},{1,17},{... | collective-permute-start | bytes 2359304 | tf_op jit(solution)/shard_map/ppermute | solution.py:700
  401.7 33.1 %collective-permute-start.59 = (bf16[2,4,352,128]{3,2,1,0:T(8,128)(2,1)S(1)}, bf16[2,4,352,128]{3,2,1,0:T(8,128)(2,1)S(1)}, u32[]{:S(2)}, u32[]{:S(2)}) collective-permute-start(bf16[2,4,352,128]{3,2,1,0:T(8,128)(2,1)S(1)} %get-tuple-element.203), channel_id=1, source_target_pairs={{0,16},{4,20},{8,24},{12,28},{16,0},{20,4},{24,8},{28,12},{1,17},{... | collective-permute-start | bytes 2162696 | tf_op jit(solution)/shard_map/ppermute | solution.py:700
  420.2 40.3 %collective-permute-start.29 = (bf16[2,4,384,128]{3,2,1,0:T(8,128)(2,1)S(1)}, bf16[2,4,384,128]{3,2,1,0:T(8,128)(2,1)S(1)}, u32[]{:S(2)}, u32[]{:S(2)}) collective-permute-start(bf16[2,4,384,128]{3,2,1,0:T(8,128)(2,1)S(1)} %get-tuple-element.199), channel_id=1, source_target_pairs={{0,16},{4,20},{8,24},{12,28},{16,0},{20,4},{24,8},{28,12},{1,17},{... | collective-permute-start | bytes 2359304 | tf_op jit(solution)/shard_map/ppermute | solution.py:700
  436.6 23.0 %collective-permute-start.20 = (bf16[1,4,384,128]{3,2,1,0:T(8,128)(2,1)S(1)}, bf16[1,4,384,128]{3,2,1,0:T(8,128)(2,1)S(1)}, u32[]{:S(2)}, u32[]{:S(2)}) collective-permute-start(bf16[1,4,384,128]{3,2,1,0:T(8,128)(2,1)S(1)} %add_convert_fusion.27), channel_id=1, source_target_pairs={{0,16},{4,20},{8,24},{12,28},{16,0},{20,4},{24,8},{28,12},{1,17},{... | collective-permute-start | bytes 1179656 | tf_op jit(solution)/shard_map/ppermute | solution.py:700
  445.0 87.2 %collective-permute-start.44 = (bf16[256,128]{1,0:T(8,128)(2,1)S(1)}, bf16[256,128]{1,0:T(8,128)(2,1)S(1)}, u32[]{:S(2)}, u32[]{:S(2)}) collective-permute-start(bf16[256,128]{1,0:T(8,128)(2,1)S(1)} %get-tuple-element.245), channel_id=1, source_target_pairs={{0,1},{1,2},{4,5},{5,6},{8,9},{9,10},{12,13},{13,14},{16,17},{17,1... | collective-permute-start | bytes 196616 | tf_op jit(solution)/shard_map/ppermute | solution.py:752
  464.3 36.9 %collective-permute-start.53 = (bf16[2,4,704,128]{3,2,1,0:T(8,128)(2,1)S(1)}, bf16[2,4,704,128]{3,2,1,0:T(8,128)(2,1)S(1)}, u32[]{:S(2)}, u32[]{:S(2)}) collective-permute-start(bf16[2,4,704,128]{3,2,1,0:T(8,128)(2,1)S(1)} %get-tuple-element.197), channel_id=1, source_target_pairs={{0,16},{4,20},{8,24},{12,28},{16,0},{20,4},{24,8},{28,12},{1,17},{... | collective-permute-start | bytes 4325384 | tf_op jit(solution)/shard_map/ppermute | solution.py:700
  470.9 38.0 %collective-permute-start.50 = (bf16[2,4,704,128]{3,2,1,0:T(8,128)(2,1)S(1)}, bf16[2,4,704,128]{3,2,1,0:T(8,128)(2,1)S(1)}, u32[]{:S(2)}, u32[]{:S(2)}) collective-permute-start(bf16[2,4,704,128]{3,2,1,0:T(8,128)(2,1)S(1)} %get-tuple-element.195), channel_id=1, source_target_pairs={{0,8},{4,12},{8,0},{12,4},{16,24},{20,28},{24,16},{28,20},{1,9},{5... | collective-permute-start | bytes 4325384 | tf_op jit(solution)/shard_map/ppermute | solution.py:700
  471.9 60.3 %collective-permute-start.47 = (bf16[256,128]{1,0:T(8,128)(2,1)S(1)}, bf16[256,128]{1,0:T(8,128)(2,1)S(1)}, u32[]{:S(2)}, u32[]{:S(2)}) collective-permute-start(bf16[256,128]{1,0:T(8,128)(2,1)S(1)} %get-tuple-element.246), channel_id=1, source_target_pairs={{3,2},{2,1},{7,6},{6,5},{11,10},{10,9},{15,14},{14,13},{19,18},{18... | collective-permute-start | bytes 196616 | tf_op jit(solution)/shard_map/ppermute | solution.py:752
  479.6 30.2 %collective-permute-start.31 = (bf16[1280,128]{1,0:T(8,128)(2,1)S(1)}, bf16[1280,128]{1,0:T(8,128)(2,1)S(1)}, u32[]{:S(2)}, u32[]{:S(2)}) collective-permute-start(bf16[1280,128]{1,0:T(8,128)(2,1)S(1)} %get-tuple-element.214), channel_id=1, source_target_pairs={{0,1},{4,5},{8,9},{12,13},{16,17},{20,21},{24,25},{28,29}} | collective-permute-start | bytes 983048 | tf_op jit(solution)/shard_map/ppermute | solution.py:752
  501.2 36.9 %collective-permute-start.34 = (bf16[1280,128]{1,0:T(8,128)(2,1)S(1)}, bf16[1280,128]{1,0:T(8,128)(2,1)S(1)}, u32[]{:S(2)}, u32[]{:S(2)}) collective-permute-start(bf16[1280,128]{1,0:T(8,128)(2,1)S(1)} %get-tuple-element.215), channel_id=1, source_target_pairs={{3,2},{7,6},{11,10},{15,14},{19,18},{23,22},{27,26},{31,30}} | collective-permute-start | bytes 983048 | tf_op jit(solution)/shard_map/ppermute | solution.py:752
  (107 other events, 857.7 us)

commit v2 on v1

--- a/solution.py
+++ b/solution.py
@@ -988,8 +988,9 @@
     pairs_b = first_swap([memory_b], 0)
     memory_a = whole_of(later_stages(pairs_a, order_a[1:]))
     memory_b = whole_of(later_stages(pairs_b, order_b[1:]))
-    (rest_a, rest_b), (self_a, self_b) = members_sum([(rest_a, rest_b), (self_a, self_b)])
-    ((memory_a, memory_b),) = members_sum([(memory_a, memory_b)])
+    (rest_a, rest_b), (self_a, self_b), (memory_a, memory_b) = members_sum(
+        [(rest_a, rest_b), (self_a, self_b), (memory_a, memory_b)]
+    )
     tile_rows = share * (width // LANES)
     g_c_out = rows_out(rest_a, share, width, 0)
     g_c_query = rows_out(rest_b, share, width, 0)

time: 597 us -> 593 us (level)
  waiting for transfers between devices: 187 us -> 151 us
  starting transfers between devices: 101 us -> 130 us
    ppermute x12, waiting for transfers between devices: 37 us -> 14.9 us  [shifted(): lax.ppermute(array, 'mem', [(i, (i + shift) % members) for i in range(mem...]
    ppermute x12, starting transfers between devices: 19.2 us -> 40.8 us  [shifted(): lax.ppermute(array, 'mem', [(i, (i + shift) % members) for i in range(mem...]
    ppermute x32, waiting for transfers between devices: 120 us -> 103 us  [swap(): return lax.ppermute(array, 'dp', [(i, i ^ 1 << bit) for i in range(size)])]
    ppermute x32, starting transfers between devices: 23.3 us -> 29.9 us  [swap(): return lax.ppermute(array, 'dp', [(i, i ^ 1 << bit) for i in range(size)])]
    convert_element_type x30 -> x28, other arithmetic: 11.1 us -> 15.2 us  [add16(): (left.astype(jnp.float32) + right.astype(jnp.float32)).astype(jnp.bfloat16)]
    ppermute x18 -> x12, starting transfers between devices: 34 us -> 36.7 us  [along_members(): got[side] = lax.ppermute(sent, 'mem', pairs)]
    ppermute x18 -> x12, waiting for transfers between devices: 24.9 us -> 23.6 us  [along_members(): got[side] = lax.ppermute(sent, 'mem', pairs)]
  transfers between devices with their start and end apart: 67 -> 61, of which waited for: 27 -> 22; matrix products, arithmetic and copies ran while one was open for 10% -> 11% of each run, Pallas kernels for 22% -> 22%
where the time goes in v2:
time: 593 us; the launch traced here: 583 us
  Pallas kernels  195 us (33%)
  waiting for transfers between devices  151 us (25%)
  starting transfers between devices  130 us (22%)
  other arithmetic  45.1 us (8%)
  matrix products  41.8 us (7%)
  local copies, waits for them, and re-layouts  18.3 us (3%)
    ppermute x32, waiting for transfers between devices, swap(): return lax.ppermute(array, 'dp', [(i, i ^ 1 << bit) for i in range(size)])  103 us
    pallas_call x7, Pallas kernels, outer_arranged(): pl.pallas_call(kernel, out_shape=tuple(out_shape), grid_spec=pltpu.Prefet...  44.3 us
    dot_general x18, matrix products, dot32(): lax.dot_general(left, right, (dims, ((), ())), preferred_element_type=jnp...  41.2 us
    ppermute x12, starting transfers between devices, shifted(): lax.ppermute(array, 'mem', [(i, (i + shift) % members) for i in range(mem...  40.8 us
    ppermute x12, starting transfers between devices, along_members(): got[side] = lax.ppermute(sent, 'mem', pairs)  36.7 us
    pallas_call x2, Pallas kernels, feed_forward(): pl.pallas_call(feed_forward_kernel, out_shape=(shape((rows, hidden), jnp....  34.6 us
    pallas_call x2, Pallas kernels, cross_attention_back(): pl.pallas_call(functools.partial(cross_backward_kernel, chunks), out_shap...  34.3 us
    ppermute x32, starting transfers between devices, swap(): return lax.ppermute(array, 'dp', [(i, i ^ 1 << bit) for i in range(size)])  29.9 us
  transfers between devices with their start and end apart: 61, of which 22 were waited for; matrix products, arithmetic and copies ran while one was open for 11% of the time, Pallas kernels for 22%

profile of v2, /device:TPU:0, one launch (start us, length us, event | category | flops | bytes accessed | tf_op | source)
XLA Modules:
  0.0 582.6 jit_solution(13577001304128651318)
XLA Ops:
  0.7 6.6 %shard_map.359 = (bf16[1,256,1024]{2,1,0:T(8,128)(2,1)}, bf16[1,256,1024]{2,1,0:T(8,128)(2,1)}, bf16[1,256,1024]{2,1,0:T(8,128)(2,1)}, bf16[1,256,1024]{2,1,0:T(8,128)(2,1)}) custom-call(s32[1]{0:T(128)} %bitcast.10.place_ref, bf16[2,4,256,1024]{3,2,1,0:T(8,128)(2,1)} %x_ref.5, bf16[1024,512]{1,0:T(8,128)(2,1)} %ck_ref.5, bf16[1024,512]{1,0:T(8,128)(2,1)} %cv_ref.5), custom_call_target="tpu_custom_call" | custom-call | tf_op jit(solution)/shard_map/pallas_call | solution.py:602
  14.2 6.4 %shard_map.362 = (bf16[1,256,1024]{2,1,0:T(8,128)(2,1)}, bf16[1,256,1024]{2,1,0:T(8,128)(2,1)}, bf16[1,256,1024]{2,1,0:T(8,128)(2,1)}, bf16[1,256,1024]{2,1,0:T(8,128)(2,1)}) custom-call(s32[1]{0:T(128)} %bitcast.10.place_ref, bf16[2,4,256,1024]{3,2,1,0:T(8,128)(2,1)} %x_ref.5, bf16[1024,512]{1,0:T(8,128)(2,1)} %ck_ref.5, bf16[1024,512]{1,0:T(8,128)(2,1)} %cv_ref.5), custom_call_target="tpu_custom_call" | custom-call | tf_op jit(solution)/shard_map/pallas_call | solution.py:602
  31.1 14.6 %shard_map.358 = (bf16[512,1024]{1,0:T(8,128)(2,1)}, f32[2,4,8,256]{3,2,1,0:T(8,128)}) custom-call(s32[2]{0:T(128)} %bitcast.292, bf16[512,1024]{1,0:T(8,128)(2,1)} %convolution_convert_fusion.q_ref, bf16[512,512]{1,0:T(8,128)(2,1)} %convolution_convert_fusion.8.k_ref, bf16[512,512]{1,0:T(8,128)(2,1)} %convolution_convert_fusion.7.v_ref, ...), custom_call_target="tpu_custom_call" | custom-call | tf_op jit(solution)/shard_map/pallas_call | solution.py:303
  63.1 12.2 %shard_map.360 = (bf16[256,1024]{1,0:T(8,128)(2,1)}, f32[1,4,8,256]{3,2,1,0:T(8,128)}) custom-call(s32[1]{0:T(128)} %bitcast.5.count_ref, s32[4]{0:T(128)} %pad_add_fusion.base_ref, bf16[256,1024]{1,0:T(8,128)(2,1)} %convolution_convert_fusion.6.q_ref, bf16[1,256,1024]{2,1,0:T(8,128)(2,1)} %get-tuple-element.82.refs_0_.refs_4_, ...), custom_call_target="tpu_custom_call" | custom-call | tf_op jit(solution)/shard_map/pallas_call | solution.py:365
  80.0 17.3 %shard_map.361 = (bf16[256,2816]{1,0:T(8,128)(2,1)}, bf16[256,2816]{1,0:T(8,128)(2,1)}, bf16[256,2816]{1,0:T(8,128)(2,1)}, f32[256,1024]{1,0:T(8,128)}, f32[256,1024]{1,0:T(8,128)}) custom-call(bf16[256,1024]{1,0:T(8,128)(2,1)} %multiply_convert_fusion.2.n_ref.refs_0_, bf16[256,1024]{1,0:T(8,128)(2,1)} %get-tuple-element.234.b_ref.refs_2_.refs_4_, ...), custom_call_target="tpu_custom_call" | custom-call | tf_op jit(solution)/shard_map/pallas_call | solution.py:410
  102.7 17.1 %shard_map.365 = (bf16[256,1024]{1,0:T(8,128)(2,1)}, bf16[1,256,1024]{2,1,0:T(8,128)(2,1)}, bf16[1,256,1024]{2,1,0:T(8,128)(2,1)}, bf16[1,256,1024]{2,1,0:T(8,128)(2,1)}, bf16[1,256,1024]{2,1,0:T(8,128)(2,1)}) custom-call(s32[1]{0:T(128)} %bitcast.5.count_ref, s32[4]{0:T(128)} %pad_add_fusion.base_ref, bf16[256,1024]{1,0:T(8,128)(2,1)} %convolution_convert_fusion.6.q_ref, ...), custom_call_target="tpu_custom_call" | custom-call | tf_op jit(solution)/shard_map/pallas_call | solution.py:384
  125.5 12.4 %shard_map.363 = (bf16[256,1024]{1,0:T(8,128)(2,1)}, f32[1,4,8,256]{3,2,1,0:T(8,128)}) custom-call(s32[1]{0:T(128)} %bitcast.15.count_ref, s32[4]{0:T(128)} %pad_add_fusion.base_ref, bf16[256,1024]{1,0:T(8,128)(2,1)} %convolution_convert_fusion.5.q_ref, bf16[1,256,1024]{2,1,0:T(8,128)(2,1)} %get-tuple-element.88.refs_0_.refs_4_, ...), custom_call_target="tpu_custom_call" | custom-call | tf_op jit(solution)/shard_map/pallas_call | solution.py:365
  144.3 17.3 %shard_map.364 = (bf16[256,2816]{1,0:T(8,128)(2,1)}, bf16[256,2816]{1,0:T(8,128)(2,1)}, bf16[256,2816]{1,0:T(8,128)(2,1)}, f32[256,1024]{1,0:T(8,128)}, f32[256,1024]{1,0:T(8,128)}) custom-call(bf16[256,1024]{1,0:T(8,128)(2,1)} %get-tuple-element.248.n_ref.refs_1_, bf16[256,1024]{1,0:T(8,128)(2,1)} %get-tuple-element.235.b_ref.refs_3_.refs_5_, ...), custom_call_target="tpu_custom_call" | custom-call | tf_op jit(solution)/shard_map/pallas_call | solution.py:410
  167.1 17.2 %shard_map.366 = (bf16[256,1024]{1,0:T(8,128)(2,1)}, bf16[1,256,1024]{2,1,0:T(8,128)(2,1)}, bf16[1,256,1024]{2,1,0:T(8,128)(2,1)}, bf16[1,256,1024]{2,1,0:T(8,128)(2,1)}, bf16[1,256,1024]{2,1,0:T(8,128)(2,1)}) custom-call(s32[1]{0:T(128)} %bitcast.15.count_ref, s32[4]{0:T(128)} %pad_add_fusion.base_ref, bf16[256,1024]{1,0:T(8,128)(2,1)} %convolution_convert_fusion.5.q_ref, ...), custom_call_target="tpu_custom_call" | custom-call | tf_op jit(solution)/shard_map/pallas_call | solution.py:384
  191.4 12.1 %shard_map.367 = (bf16[512,1024]{1,0:T(8,128)(2,1)}, bf16[512,512]{1,0:T(8,128)(2,1)}, bf16[512,512]{1,0:T(8,128)(2,1)}, f32[2,4,4,256]{3,2,1,0:T(4,128)}) custom-call(s32[2]{0:T(128)} %bitcast.293, bf16[512,1024]{1,0:T(8,128)(2,1)} %convolution_convert_fusion.q_ref, bf16[512,512]{1,0:T(8,128)(2,1)} %convolution_convert_fusion.8.k_ref, ...), custom_call_target="tpu_custom_call" | custom-call | tf_op jit(solution)/shard_map/pallas_call | solution.py:326
  203.5 4.6 fusion.58
  210.8 4.9 fusion.7
  215.7 18.4 %collective-permute-start.12 = (f32[3584]{0:T(1024)S(1)}, f32[3584]{0:T(1024)S(1)}, u32[]{:S(2)}, u32[]{:S(2)}) collective-permute-start(f32[3584]{0:T(1024)S(1)} %pad_maximum_fusion.8), channel_id=1, source_target_pairs={{0,1},{1,0},{2,3},{3,2},{4,5},{5,4},{6,7},{7,6},{8,9},{9,8},{10,11... | collective-permute-start | bytes 43016 | tf_op jit(solution)/shard_map/ppermute | solution.py:774
  238.7 9.5 %collective-permute-done.13 = f32[3584]{0:T(1024)S(1)} collective-permute-done((f32[3584]{0:T(1024)S(1)}, f32[3584]{0:T(1024)S(1)}, u32[]{:S(2)}, u32[]{:S(2)}) %collective-permute-start.13) | collective-permute-done | bytes 14368 | tf_op jit(solution)/shard_map/ppermute | solution.py:774
  253.8 6.8 %shard_map.372 = (bf16[4,4,128,128]{3,2,1,0:T(8,128)(2,1)}, bf16[4,4,128,128]{3,2,1,0:T(8,128)(2,1)}, bf16[4,4,384,128]{3,2,1,0:T(8,128)(2,1)}, bf16[4,4,384,128]{3,2,1,0:T(8,128)(2,1)}) custom-call(s32[1]{0:T(128)} %bitcast.23.me_ref, bf16[512,1024]{1,0:T(8,128)(2,1)} %copy-done.28, bf16[512,512]{1,0:T(8,128)(2,1)} %get-tuple-element.102.refs_1_, ...), custom_call_target="tpu_custom_call" | custom-call | tf_op jit(solution)/shard_map/pallas_call | solution.py:566
  261.7 4.8 shard_map.370
  271.8 14.9 %collective-permute-done.7.refs_2_ = bf16[1,256,1024]{2,1,0:T(8,128)(2,1)S(1)} collective-permute-done((bf16[1,256,1024]{2,1,0:T(8,128)(2,1)}, bf16[1,256,1024]{2,1,0:T(8,128)(2,1)S(1)}, u32[]{:S(2)}, u32[]{:S(2)}) %collective-permute-start.7) | collective-permute-done | bytes 524320 | tf_op jit(solution)/shard_map/ppermute | solution.py:815
  286.7 21.8 %collective-permute-start.11 = (bf16[1,256,1024]{2,1,0:T(8,128)(2,1)}, bf16[1,256,1024]{2,1,0:T(8,128)(2,1)}, u32[]{:S(2)}, u32[]{:S(2)}) collective-permute-start(bf16[1,256,1024]{2,1,0:T(8,128)(2,1)} %get-tuple-element.111), channel_id=1, source_target_pairs={{0,1},{1,2},{2,3},{3,0},{4,5},{5,6},{6,7},{7,4},{8,9},{9,10},{10,1... | collective-permute-start | bytes 1572872 | tf_op jit(solution)/shard_map/ppermute | solution.py:815
  309.1 4.7 shard_map.371
  313.8 9.2 %shard_map.375 = (bf16[4,4,352,128]{3,2,1,0:T(8,128)(2,1)}, bf16[4,4,352,128]{3,2,1,0:T(8,128)(2,1)}, bf16[4,4,352,128]{3,2,1,0:T(8,128)(2,1)}, bf16[4,4,352,128]{3,2,1,0:T(8,128)(2,1)}) custom-call(s32[1]{0:T(128)} %bitcast.23.me_ref, bf16[256,2816]{1,0:T(8,128)(2,1)} %get-tuple-element.138.refs_0_, bf16[256,2816]{1,0:T(8,128)(2,1)} %get-tuple-element.139.refs_1_, ...), custom_call_target="tpu_custom_call" | custom-call | tf_op jit(solution)/shard_map/pallas_call | solution.py:566
  323.0 7.3 %shard_map.374 = (bf16[4,4,704,128]{3,2,1,0:T(8,128)(2,1)}, bf16[4,4,704,128]{3,2,1,0:T(8,128)(2,1)}) custom-call(s32[1]{0:T(128)} %bitcast.23.me_ref, bf16[256,1024]{1,0:T(8,128)(2,1)} %multiply_convert_fusion.2.n_ref.refs_0_, bf16[256,1024]{1,0:T(8,128)(2,1)} %get-tuple-element.248.n_ref.refs_1_, bf16[256,2816]{1,0:T(8,128)(2,1)} %get-tuple-element.134.refs_2_, ...), custom_call_target="tpu_custom_call" | custom-call | tf_op jit(solution)/shard_map/pallas_call | solution.py:566
  330.3 7.4 %shard_map.373 = (bf16[4,4,704,128]{3,2,1,0:T(8,128)(2,1)}, bf16[4,4,704,128]{3,2,1,0:T(8,128)(2,1)}) custom-call(s32[1]{0:T(128)} %bitcast.23.me_ref, bf16[256,1024]{1,0:T(8,128)(2,1)} %multiply_convert_fusion.2.n_ref.refs_0_, bf16[256,1024]{1,0:T(8,128)(2,1)} %get-tuple-element.248.n_ref.refs_1_, bf16[256,2816]{1,0:T(8,128)(2,1)} %get-tuple-element.130.refs_2_, ...), custom_call_target="tpu_custom_call" | custom-call | tf_op jit(solution)/shard_map/pallas_call | solution.py:566
  343.6 17.3 %shard_map.368 = (bf16[2,4,256,1024]{3,2,1,0:T(8,128)(2,1)}, bf16[4,4,128,128]{3,2,1,0:T(8,128)(2,1)}, bf16[4,4,128,128]{3,2,1,0:T(8,128)(2,1)}, bf16[4,4,128,12...) custom-call(s32[2]{0:T(128)} %pad_add_fusion.1.place_ref, bf16[2,4,256,1024]{3,2,1,0:T(8,128)(2,1)} %x_ref.5, ...), custom_call_target="tpu_custom_call" | custom-call | tf_op jit(solution)/shard_map/pallas_call | solution.py:675
  382.4 13.3 %collective-permute-done.19 = bf16[2,4,384,128]{3,2,1,0:T(8,128)(2,1)S(1)} collective-permute-done((bf16[2,4,384,128]{3,2,1,0:T(8,128)(2,1)S(1)}, bf16[2,4,384,128]{3,2,1,0:T(8,128)(2,1)S(1)}, u32[]{:S(2)}, u32[]{:S(2)}) %collective-permute-start.19) | collective-permute-done | bytes 786464 | tf_op jit(solution)/shard_map/ppermute | solution.py:700
  399.7 13.8 %collective-permute-done.53 = bf16[2,4,352,128]{3,2,1,0:T(8,128)(2,1)S(1)} collective-permute-done((bf16[2,4,352,128]{3,2,1,0:T(8,128)(2,1)S(1)}, bf16[2,4,352,128]{3,2,1,0:T(8,128)(2,1)S(1)}, u32[]{:S(2)}, u32[]{:S(2)}) %collective-permute-start.53) | collective-permute-done | bytes 720928 | tf_op jit(solution)/shard_map/ppermute | solution.py:700
  416.1 22.0 %collective-permute-done.20 = bf16[1,4,384,128]{3,2,1,0:T(8,128)(2,1)S(1)} collective-permute-done((bf16[1,4,384,128]{3,2,1,0:T(8,128)(2,1)S(1)}, bf16[1,4,384,128]{3,2,1,0:T(8,128)(2,1)S(1)}, u32[]{:S(2)}, u32[]{:S(2)}) %collective-permute-start.20) | collective-permute-done | bytes 393248 | tf_op jit(solution)/shard_map/ppermute | solution.py:700
  447.1 5.1 collective-permute-done.54
  457.9 5.6 collective-permute-done.51
  467.1 28.6 %collective-permute-done.36 = bf16[1,4,128,128]{3,2,1,0:T(8,128)(2,1)S(1)} collective-permute-done((bf16[1,4,128,128]{3,2,1,0:T(8,128)(2,1)S(1)}, bf16[1,4,128,128]{3,2,1,0:T(8,128)(2,1)S(1)}, u32[]{:S(2)}, u32[]{:S(2)}) %collective-permute-start.36) | collective-permute-done | bytes 131104 | tf_op jit(solution)/shard_map/ppermute | solution.py:700
  495.8 14.4 %collective-permute-start.37 = (bf16[1536,128]{1,0:T(8,128)(2,1)S(1)}, bf16[1536,128]{1,0:T(8,128)(2,1)S(1)}, u32[]{:S(2)}, u32[]{:S(2)}) collective-permute-start(bf16[1536,128]{1,0:T(8,128)(2,1)S(1)} %get-tuple-element.214), channel_id=1, source_target_pairs={{0,1},{4,5},{8,9},{12,13},{16,17},{20,21},{24,25},{28,29}} | collective-permute-start | bytes 1179656 | tf_op jit(solution)/shard_map/ppermute | solution.py:752
  547.0 5.7 collective-permute-done.56
  571.2 7.1 %collective-permute-done.60 = bf16[2112,128]{1,0:T(8,128)(2,1)S(1)} collective-permute-done((bf16[2112,128]{1,0:T(8,128)(2,1)S(1)}, bf16[2112,128]{1,0:T(8,128)(2,1)S(1)}, u32[]{:S(2)}, u32[]{:S(2)}) %collective-permute-start.60) | collective-permute-done | bytes 540704 | tf_op jit(solution)/shard_map/ppermute | solution.py:752
  (398 shorter events, 200.0 us)
Async XLA Ops:
  7.2 52.6 %collective-permute-start = (bf16[1,256,1024]{2,1,0:T(8,128)(2,1)}, bf16[1,256,1024]{2,1,0:T(8,128)(2,1)}, u32[]{:S(2)}, u32[]{:S(2)}) collective-permute-start(bf16[1,256,1024]{2,1,0:T(8,128)(2,1)} %get-tuple-element.83), channel_id=1, source_target_pairs={{0,1},{1,2},{2,3},{3,0},{4,5},{5,6},{6,7},{7,4},{8,9},{9,10},{10,1... | collective-permute-start | bytes 1572872 | tf_op jit(solution)/shard_map/ppermute | solution.py:815
  10.3 52.8 %collective-permute-start.1 = (bf16[1,256,1024]{2,1,0:T(8,128)(2,1)}, bf16[1,256,1024]{2,1,0:T(8,128)(2,1)}, u32[]{:S(2)}, u32[]{:S(2)}) collective-permute-start(bf16[1,256,1024]{2,1,0:T(8,128)(2,1)} %get-tuple-element.84), channel_id=1, source_target_pairs={{0,2},{1,3},{2,0},{3,1},{4,6},{5,7},{6,4},{7,5},{8,10},{9,11},{10,... | collective-permute-start | bytes 1572872 | tf_op jit(solution)/shard_map/ppermute | solution.py:815
  12.9 50.2 %collective-permute-start.2 = (bf16[1,256,1024]{2,1,0:T(8,128)(2,1)}, bf16[1,256,1024]{2,1,0:T(8,128)(2,1)}, u32[]{:S(2)}, u32[]{:S(2)}) collective-permute-start(bf16[1,256,1024]{2,1,0:T(8,128)(2,1)} %get-tuple-element.85), channel_id=1, source_target_pairs={{0,3},{1,0},{2,1},{3,2},{4,7},{5,4},{6,5},{7,6},{8,11},{9,8},{10,9... | collective-permute-start | bytes 1572872 | tf_op jit(solution)/shard_map/ppermute | solution.py:815
  20.6 104.9 %collective-permute-start.3 = (bf16[1,256,1024]{2,1,0:T(8,128)(2,1)}, bf16[1,256,1024]{2,1,0:T(8,128)(2,1)}, u32[]{:S(2)}, u32[]{:S(2)}) collective-permute-start(bf16[1,256,1024]{2,1,0:T(8,128)(2,1)} %get-tuple-element.89), channel_id=1, source_target_pairs={{0,1},{1,2},{2,3},{3,0},{4,5},{5,6},{6,7},{7,4},{8,9},{9,10},{10,1... | collective-permute-start | bytes 1572872 | tf_op jit(solution)/shard_map/ppermute | solution.py:815
  21.3 104.2 %collective-permute-start.4 = (bf16[1,256,1024]{2,1,0:T(8,128)(2,1)}, bf16[1,256,1024]{2,1,0:T(8,128)(2,1)}, u32[]{:S(2)}, u32[]{:S(2)}) collective-permute-start(bf16[1,256,1024]{2,1,0:T(8,128)(2,1)} %get-tuple-element.90), channel_id=1, source_target_pairs={{0,2},{1,3},{2,0},{3,1},{4,6},{5,7},{6,4},{7,5},{8,10},{9,11},{10,... | collective-permute-start | bytes 1572872 | tf_op jit(solution)/shard_map/ppermute | solution.py:815
  59.8 65.7 %collective-permute-start.5 = (bf16[1,256,1024]{2,1,0:T(8,128)(2,1)}, bf16[1,256,1024]{2,1,0:T(8,128)(2,1)}, u32[]{:S(2)}, u32[]{:S(2)}) collective-permute-start(bf16[1,256,1024]{2,1,0:T(8,128)(2,1)} %get-tuple-element.91), channel_id=1, source_target_pairs={{0,3},{1,0},{2,1},{3,2},{4,7},{5,4},{6,5},{7,6},{8,11},{9,8},{10,9... | collective-permute-start | bytes 1572872 | tf_op jit(solution)/shard_map/ppermute | solution.py:815
  215.7 20.6 %collective-permute-start.12 = (f32[3584]{0:T(1024)S(1)}, f32[3584]{0:T(1024)S(1)}, u32[]{:S(2)}, u32[]{:S(2)}) collective-permute-start(f32[3584]{0:T(1024)S(1)} %pad_maximum_fusion.8), channel_id=1, source_target_pairs={{0,1},{1,0},{2,3},{3,2},{4,5},{5,4},{6,7},{7,6},{8,9},{9,8},{10,11... | collective-permute-start | bytes 43016 | tf_op jit(solution)/shard_map/ppermute | solution.py:774
  234.2 32.3 %collective-permute-start.6 = (bf16[1,256,1024]{2,1,0:T(8,128)(2,1)}, bf16[1,256,1024]{2,1,0:T(8,128)(2,1)S(1)}, u32[]{:S(2)}, u32[]{:S(2)}) collective-permute-start(bf16[1,256,1024]{2,1,0:T(8,128)(2,1)} %get-tuple-element.105), channel_id=1, source_target_pairs={{0,3},{1,0},{2,1},{3,2},{4,7},{5,4},{6,5},{7,6},{8,11},{9,8},{10,9... | collective-permute-start | bytes 1572872 | tf_op jit(solution)/shard_map/ppermute | solution.py:815
  248.2 38.5 %collective-permute-start.7 = (bf16[1,256,1024]{2,1,0:T(8,128)(2,1)}, bf16[1,256,1024]{2,1,0:T(8,128)(2,1)S(1)}, u32[]{:S(2)}, u32[]{:S(2)}) collective-permute-start(bf16[1,256,1024]{2,1,0:T(8,128)(2,1)} %get-tuple-element.106), channel_id=1, source_target_pairs={{0,2},{1,3},{2,0},{3,1},{4,6},{5,7},{6,4},{7,5},{8,10},{9,11},{10,... | collective-permute-start | bytes 1572872 | tf_op jit(solution)/shard_map/ppermute | solution.py:815
  249.9 36.8 %collective-permute-start.8 = (bf16[1,256,1024]{2,1,0:T(8,128)(2,1)}, bf16[1,256,1024]{2,1,0:T(8,128)(2,1)}, u32[]{:S(2)}, u32[]{:S(2)}) collective-permute-start(bf16[1,256,1024]{2,1,0:T(8,128)(2,1)} %get-tuple-element.107), channel_id=1, source_target_pairs={{0,1},{1,2},{2,3},{3,0},{4,5},{5,6},{6,7},{7,4},{8,9},{9,10},{10,1... | collective-permute-start | bytes 1572872 | tf_op jit(solution)/shard_map/ppermute | solution.py:815
  253.1 55.4 %collective-permute-start.9 = (bf16[1,256,1024]{2,1,0:T(8,128)(2,1)}, bf16[1,256,1024]{2,1,0:T(8,128)(2,1)}, u32[]{:S(2)}, u32[]{:S(2)}) collective-permute-start(bf16[1,256,1024]{2,1,0:T(8,128)(2,1)} %get-tuple-element.109), channel_id=1, source_target_pairs={{0,3},{1,0},{2,1},{3,2},{4,7},{5,4},{6,5},{7,6},{8,11},{9,8},{10,9... | collective-permute-start | bytes 1572872 | tf_op jit(solution)/shard_map/ppermute | solution.py:815
  260.6 48.1 %collective-permute-start.25 = (bf16[4,4,128,128]{3,2,1,0:T(8,128)(2,1)}, bf16[4,4,128,128]{3,2,1,0:T(8,128)(2,1)}, u32[]{:S(2)}, u32[]{:S(2)}) collective-permute-start(bf16[4,4,128,128]{3,2,1,0:T(8,128)(2,1)} %get-tuple-element.123), channel_id=1, source_target_pairs={{0,4},{4,0},{8,12},{12,8},{16,20},{20,16},{24,28},{28,24},{1,5},{5... | collective-permute-start | bytes 1572872 | tf_op jit(solution)/shard_map/ppermute | solution.py:700
  266.5 73.0 %collective-permute-start.18 = (bf16[4,4,128,128]{3,2,1,0:T(8,128)(2,1)}, bf16[4,4,128,128]{3,2,1,0:T(8,128)(2,1)}, u32[]{:S(2)}, u32[]{:S(2)}) collective-permute-start(bf16[4,4,128,128]{3,2,1,0:T(8,128)(2,1)} %get-tuple-element.117), channel_id=1, source_target_pairs={{0,4},{4,0},{8,12},{12,8},{16,20},{20,16},{24,28},{28,24},{1,5},{5... | collective-permute-start | bytes 1572872 | tf_op jit(solution)/shard_map/ppermute | solution.py:700
  286.7 56.4 %collective-permute-start.10 = (bf16[1,256,1024]{2,1,0:T(8,128)(2,1)}, bf16[1,256,1024]{2,1,0:T(8,128)(2,1)}, u32[]{:S(2)}, u32[]{:S(2)}) collective-permute-start(bf16[1,256,1024]{2,1,0:T(8,128)(2,1)} %get-tuple-element.110), channel_id=1, source_target_pairs={{0,2},{1,3},{2,0},{3,1},{4,6},{5,7},{6,4},{7,5},{8,10},{9,11},{10,... | collective-permute-start | bytes 1572872 | tf_op jit(solution)/shard_map/ppermute | solution.py:815
  286.7 56.4 %collective-permute-start.11 = (bf16[1,256,1024]{2,1,0:T(8,128)(2,1)}, bf16[1,256,1024]{2,1,0:T(8,128)(2,1)}, u32[]{:S(2)}, u32[]{:S(2)}) collective-permute-start(bf16[1,256,1024]{2,1,0:T(8,128)(2,1)} %get-tuple-element.111), channel_id=1, source_target_pairs={{0,1},{1,2},{2,3},{3,0},{4,5},{5,6},{6,7},{7,4},{8,9},{9,10},{10,1... | collective-permute-start | bytes 1572872 | tf_op jit(solution)/shard_map/ppermute | solution.py:815
  308.5 54.3 %collective-permute-start.17 = (bf16[4,4,256,128]{3,2,1,0:T(8,128)(2,1)}, bf16[4,4,256,128]{3,2,1,0:T(8,128)(2,1)S(1)}, u32[]{:S(2)}, u32[]{:S(2)}) collective-permute-start(bf16[4,4,256,128]{3,2,1,0:T(8,128)(2,1)} %get-tuple-element.115), channel_id=1, source_target_pairs={{0,4},{4,0},{8,12},{12,8},{16,20},{20,16},{24,28},{28,24},{1,5},{5... | collective-permute-start | bytes 3145736 | tf_op jit(solution)/shard_map/ppermute | solution.py:700
  308.6 52.3 %collective-permute-start.22 = (bf16[4,4,128,128]{3,2,1,0:T(8,128)(2,1)}, bf16[4,4,128,128]{3,2,1,0:T(8,128)(2,1)}, u32[]{:S(2)}, u32[]{:S(2)}) collective-permute-start(bf16[4,4,128,128]{3,2,1,0:T(8,128)(2,1)} %get-tuple-element.121), channel_id=1, source_target_pairs={{0,4},{4,0},{8,12},{12,8},{16,20},{20,16},{24,28},{28,24},{1,5},{5... | collective-permute-start | bytes 1572872 | tf_op jit(solution)/shard_map/ppermute | solution.py:700
  339.5 22.8 %collective-permute-start.26 = (bf16[2,4,128,128]{3,2,1,0:T(8,128)(2,1)}, bf16[2,4,128,128]{3,2,1,0:T(8,128)(2,1)S(1)}, u32[]{:S(2)}, u32[]{:S(2)}) collective-permute-start(bf16[2,4,128,128]{3,2,1,0:T(8,128)(2,1)} %get-tuple-element.225), channel_id=1, source_target_pairs={{0,8},{4,12},{8,0},{12,4},{16,24},{20,28},{24,16},{28,20},{1,9},{5... | collective-permute-start | bytes 786440 | tf_op jit(solution)/shard_map/ppermute | solution.py:700
  343.1 24.2 %collective-permute-start.21 = (bf16[4,4,256,128]{3,2,1,0:T(8,128)(2,1)}, bf16[4,4,256,128]{3,2,1,0:T(8,128)(2,1)}, u32[]{:S(2)}, u32[]{:S(2)}) collective-permute-start(bf16[4,4,256,128]{3,2,1,0:T(8,128)(2,1)} %get-tuple-element.119), channel_id=1, source_target_pairs={{0,4},{4,0},{8,12},{12,8},{16,20},{20,16},{24,28},{28,24},{1,5},{5... | collective-permute-start | bytes 3145736 | tf_op jit(solution)/shard_map/ppermute | solution.py:700
  343.1 36.5 %collective-permute-start.28 = (bf16[4,4,384,128]{3,2,1,0:T(8,128)(2,1)}, bf16[4,4,384,128]{3,2,1,0:T(8,128)(2,1)}, u32[]{:S(2)}, u32[]{:S(2)}) collective-permute-start(bf16[4,4,384,128]{3,2,1,0:T(8,128)(2,1)} %get-tuple-element.125), channel_id=1, source_target_pairs={{0,4},{4,0},{8,12},{12,8},{16,20},{20,16},{24,28},{28,24},{1,5},{5... | collective-permute-start | bytes 4718600 | tf_op jit(solution)/shard_map/ppermute | solution.py:700
  375.1 78.8 %collective-permute-start.46 = (bf16[4,4,704,128]{3,2,1,0:T(8,128)(2,1)S(1)}, bf16[4,4,704,128]{3,2,1,0:T(8,128)(2,1)S(1)}, u32[]{:S(2)}, u32[]{:S(2)}) collective-permute-start(bf16[4,4,704,128]{3,2,1,0:T(8,128)(2,1)S(1)} %copy-done.74), channel_id=1, source_target_pairs={{0,4},{4,0},{8,12},{12,8},{16,20},{20,16},{24,28},{28,24},{1,5},{5... | collective-permute-start | bytes 8650760 | tf_op jit(solution)/shard_map/ppermute | solution.py:700
  375.6 80.5 %collective-permute-start.43 = (bf16[4,4,704,128]{3,2,1,0:T(8,128)(2,1)S(1)}, bf16[4,4,704,128]{3,2,1,0:T(8,128)(2,1)S(1)}, u32[]{:S(2)}, u32[]{:S(2)}) collective-permute-start(bf16[4,4,704,128]{3,2,1,0:T(8,128)(2,1)S(1)} %copy-done.73), channel_id=1, source_target_pairs={{0,4},{4,0},{8,12},{12,8},{16,20},{20,16},{24,28},{28,24},{1,5},{5... | collective-permute-start | bytes 8650760 | tf_op jit(solution)/shard_map/ppermute | solution.py:700
  379.6 33.9 %collective-permute-start.53 = (bf16[2,4,352,128]{3,2,1,0:T(8,128)(2,1)S(1)}, bf16[2,4,352,128]{3,2,1,0:T(8,128)(2,1)S(1)}, u32[]{:S(2)}, u32[]{:S(2)}) collective-permute-start(bf16[2,4,352,128]{3,2,1,0:T(8,128)(2,1)S(1)} %get-tuple-element.203), channel_id=1, source_target_pairs={{0,16},{4,20},{8,24},{12,28},{16,0},{20,4},{24,8},{28,12},{1,17},{... | collective-permute-start | bytes 2162696 | tf_op jit(solution)/shard_map/ppermute | solution.py:700
  398.1 47.3 %collective-permute-start.29 = (bf16[2,4,384,128]{3,2,1,0:T(8,128)(2,1)S(1)}, bf16[2,4,384,128]{3,2,1,0:T(8,128)(2,1)S(1)}, u32[]{:S(2)}, u32[]{:S(2)}) collective-permute-start(bf16[2,4,384,128]{3,2,1,0:T(8,128)(2,1)S(1)} %get-tuple-element.199), channel_id=1, source_target_pairs={{0,16},{4,20},{8,24},{12,28},{16,0},{20,4},{24,8},{28,12},{1,17},{... | collective-permute-start | bytes 2359304 | tf_op jit(solution)/shard_map/ppermute | solution.py:700
  413.6 24.5 %collective-permute-start.20 = (bf16[1,4,384,128]{3,2,1,0:T(8,128)(2,1)S(1)}, bf16[1,4,384,128]{3,2,1,0:T(8,128)(2,1)S(1)}, u32[]{:S(2)}, u32[]{:S(2)}) collective-permute-start(bf16[1,4,384,128]{3,2,1,0:T(8,128)(2,1)S(1)} %add_convert_fusion.27), channel_id=1, source_target_pairs={{0,16},{4,20},{8,24},{12,28},{16,0},{20,4},{24,8},{28,12},{1,17},{... | collective-permute-start | bytes 1179656 | tf_op jit(solution)/shard_map/ppermute | solution.py:700
  415.2 23.6 %collective-permute-start.24 = (bf16[1,4,384,128]{3,2,1,0:T(8,128)(2,1)S(1)}, bf16[1,4,384,128]{3,2,1,0:T(8,128)(2,1)S(1)}, u32[]{:S(2)}, u32[]{:S(2)}) collective-permute-start(bf16[1,4,384,128]{3,2,1,0:T(8,128)(2,1)S(1)} %add_convert_fusion.24), channel_id=1, source_target_pairs={{0,8},{4,12},{8,0},{12,4},{16,24},{20,28},{24,16},{28,20},{1,9},{5... | collective-permute-start | bytes 1179656 | tf_op jit(solution)/shard_map/ppermute | solution.py:700
  438.1 91.6 %collective-permute-start.15 = (f32[3584]{0:T(1024)S(1)}, f32[3584]{0:T(1024)S(1)}, u32[]{:S(2)}, u32[]{:S(2)}) collective-permute-start(f32[3584]{0:T(1024)S(1)} %add.403), channel_id=1, source_target_pairs={{0,8},{4,12},{8,0},{12,4},{16,24},{20,28},{24,16},{28,20},{1,9},{5... | collective-permute-start | bytes 43016 | tf_op jit(solution)/shard_map/ppermute | solution.py:774
  445.4 21.5 %collective-permute-start.33 = (bf16[1,4,128,128]{3,2,1,0:T(8,128)(2,1)S(1)}, bf16[1,4,128,128]{3,2,1,0:T(8,128)(2,1)S(1)}, u32[]{:S(2)}, u32[]{:S(2)}) collective-permute-start(bf16[1,4,128,128]{3,2,1,0:T(8,128)(2,1)S(1)} %add_convert_fusion.49), channel_id=1, source_target_pairs={{0,16},{4,20},{8,24},{12,28},{16,0},{20,4},{24,8},{28,12},{1,17},{... | collective-permute-start | bytes 393224 | tf_op jit(solution)/shard_map/ppermute | solution.py:700
  456.1 54.8 %collective-permute-start.47 = (bf16[2,4,704,128]{3,2,1,0:T(8,128)(2,1)S(1)}, bf16[2,4,704,128]{3,2,1,0:T(8,128)(2,1)S(1)}, u32[]{:S(2)}, u32[]{:S(2)}) collective-permute-start(bf16[2,4,704,128]{3,2,1,0:T(8,128)(2,1)S(1)} %get-tuple-element.197), channel_id=1, source_target_pairs={{0,16},{4,20},{8,24},{12,28},{16,0},{20,4},{24,8},{28,12},{1,17},{... | collective-permute-start | bytes 4325384 | tf_op jit(solution)/shard_map/ppermute | solution.py:700
  463.5 49.0 %collective-permute-start.44 = (bf16[2,4,704,128]{3,2,1,0:T(8,128)(2,1)S(1)}, bf16[2,4,704,128]{3,2,1,0:T(8,128)(2,1)S(1)}, u32[]{:S(2)}, u32[]{:S(2)}) collective-permute-start(bf16[2,4,704,128]{3,2,1,0:T(8,128)(2,1)S(1)} %get-tuple-element.195), channel_id=1, source_target_pairs={{0,8},{4,12},{8,0},{12,4},{16,24},{20,28},{24,16},{28,20},{1,9},{5... | collective-permute-start | bytes 4325384 | tf_op jit(solution)/shard_map/ppermute | solution.py:700
  465.2 30.5 %collective-permute-start.36 = (bf16[1,4,128,128]{3,2,1,0:T(8,128)(2,1)S(1)}, bf16[1,4,128,128]{3,2,1,0:T(8,128)(2,1)S(1)}, u32[]{:S(2)}, u32[]{:S(2)}) collective-permute-start(bf16[1,4,128,128]{3,2,1,0:T(8,128)(2,1)S(1)} %add_convert_fusion.46), channel_id=1, source_target_pairs={{0,8},{4,12},{8,0},{12,4},{16,24},{20,28},{24,16},{28,20},{1,9},{5... | collective-permute-start | bytes 393224 | tf_op jit(solution)/shard_map/ppermute | solution.py:700
  495.8 21.3 %collective-permute-start.37 = (bf16[1536,128]{1,0:T(8,128)(2,1)S(1)}, bf16[1536,128]{1,0:T(8,128)(2,1)S(1)}, u32[]{:S(2)}, u32[]{:S(2)}) collective-permute-start(bf16[1536,128]{1,0:T(8,128)(2,1)S(1)} %get-tuple-element.214), channel_id=1, source_target_pairs={{0,1},{4,5},{8,9},{12,13},{16,17},{20,21},{24,25},{28,29}} | collective-permute-start | bytes 1179656 | tf_op jit(solution)/shard_map/ppermute | solution.py:752
  (106 other events, 932.1 us)
